TPU v7x, 32 devices: a whole 2x2x4 slice. The times are simulated.
32 devices in a mesh: expert: 8 (over z, x), shard: 4 (over y, core).
Axes of the slice: x: 2, y: 2, z: 4, core: 2. Of those that a mesh axis runs over, the one named last changes fastest.
Arguments:
- tokens: bfloat16 [2, 2048, 2048], P(None, ('expert', 'shard')), may hold values from -6 to 6
- cotangent: bfloat16 [2, 2048, 2048], P(None, ('expert', 'shard')), may hold values from -3 to 3
- segments: int32 [2, 8, 256], P(None, 'expert'), may hold values from 0 to 3, never falling along the last dimension, each value on 1 to 128 neighbouring positions
- routes: int32 [2, 2048, 4], P(None, ('expert', 'shard')), may hold values from 0 to 7, all different within a row; in each aligned block of 64 rows (0 to 63, 64 to 127, ..., all dimensions but the last counted through in order) at most 48 rows name the same one
- gate_weight: float32 [2, 2048, 4], P(None, ('expert', 'shard')), may hold values from 0.1 to 0.6
- gain_attn: bfloat16 [2048], P(('expert', 'shard')), may hold values from 0.5 to 1.5
- w_qkv: bfloat16 [3, 2048, 2048], P(None, 'expert', 'shard'), may hold values from -0.125 to 0.125
- b_qkv: bfloat16 [3, 16, 128], P(None, 'shard', 'expert'), may hold values from -0.59765625 to 0.59765625
- w_out: bfloat16 [2048, 2048], P('shard', 'expert'), may hold values from -0.25 to 0.25
- gain_ffn: bfloat16 [2048], P(('expert', 'shard')), may hold values from 0.5 to 1.5
- w_sgu: bfloat16 [2, 2048, 5632], P(None, 'expert', 'shard'), may hold values from -0.125 to 0.125
- w_sd: bfloat16 [5632, 2048], P('shard', 'expert'), may hold values from -0.078125 to 0.078125
- shared_gate: bfloat16 [2048], P(('expert', 'shard')), may hold values from -0.125 to 0.125
- w_egu: bfloat16 [8, 2, 2048, 1408], P('expert', None, 'shard'), may hold values from -0.125 to 0.125
- w_ed: bfloat16 [8, 1408, 2048], P('expert', 'shard'), may hold values from -0.15625 to 0.15625
Outputs:
- mixed: float32 [2, 2048, 2048], P(None, ('expert', 'shard'))
- grad_tokens: float32 [2, 2048, 2048], P(None, ('expert', 'shard'))
- grad_gate_weight: float32 [2, 2048, 4], P(None, ('expert', 'shard'))
- grad_gain_attn: float32 [2048], P(('expert', 'shard'))
- grad_w_qkv: float32 [3, 2048, 2048], P(None, 'expert', 'shard')
- grad_b_qkv: float32 [3, 16, 128], P(None, 'shard', 'expert')
- grad_w_out: float32 [2048, 2048], P('shard', 'expert')
- grad_gain_ffn: float32 [2048], P(('expert', 'shard'))
- grad_w_sgu: float32 [2, 2048, 5632], P(None, 'expert', 'shard')
- grad_w_sd: float32 [5632, 2048], P('shard', 'expert')
- grad_shared_gate: float32 [2048], P(('expert', 'shard'))
- grad_w_egu: float32 [8, 2, 2048, 1408], P('expert', None, 'shard')
- grad_w_ed: float32 [8, 1408, 2048], P('expert', 'shard')
Inputs may be any that keep to these rules, and one draw needn't show every extreme that they name: `routes`: in each micro-batch, the 64 tokens of one device name one expert at most 48 times over all their choices; a token's 4 experts differ. `segments`: documents never cross sequences; each has at most 128 tokens.
All inputs are finite; a program needn't handle non-finite values.
Results may differ from a plain program's by a relative error of at most 0.014.
Values may be sent and summed in bfloat16 or wider, within the bound.
A program may use at most 320 MiB of HBM per device.

v0:
```python
import jax
import jax.numpy as jnp
from jax import lax
from jax.sharding import PartitionSpec as P

HD = 128
FF = 1408
TOP = 4


EPSILON = 1e-06
ROPE_BASE = 1000000.0


def spread_rows(payload):
    return lax.all_gather(payload, "shard", axis=0, tiled=True)


def fold_rows(payload):
    return lax.psum_scatter(payload, "shard", scatter_dimension=0, tiled=True)


def trade_rows(payload):
    return lax.all_to_all(payload, "expert", split_axis=0, concat_axis=0, tiled=True)


def fetch_weights(vectors, w_qkv, b_qkv, w_out, w_sgu, w_sd, w_egu, w_ed):
    expert_gu, expert_down, vectors_mid = (
        lax.all_gather(w_egu, "shard", axis=2, tiled=True),
        lax.all_gather(w_ed, "shard", axis=1, tiled=True),
        lax.all_gather(vectors, "shard", axis=1, tiled=True),
    )
    mixer = (
        lax.all_gather(w_qkv, "expert", axis=1, tiled=True),
        lax.all_gather(b_qkv, "expert", axis=2, tiled=True),
        lax.all_gather(w_out, "expert", axis=1, tiled=True),
        lax.all_gather(w_sgu, "expert", axis=1, tiled=True),
        lax.all_gather(w_sd, "expert", axis=1, tiled=True),
        lax.all_gather(vectors_mid, "expert", axis=1, tiled=True),
    )
    return tuple(mixer) + (expert_gu, expert_down)


def rope_tables(length):
    position = jnp.arange(length).astype(jnp.float32)
    frequency = ROPE_BASE ** (-jnp.arange(HD // 2).astype(jnp.float32) * 2.0 / HD)
    angles = position[:, None, None] * frequency[None, None, :]
    return (jnp.cos(angles), jnp.sin(angles))


def rotate(tensor, cosine, sine):
    half_size = tensor.shape[-1] // 2
    first_half = tensor[..., :half_size]
    second_half = tensor[..., half_size:]
    return jnp.concatenate(
        [first_half * cosine - second_half * sine, first_half * sine + second_half * cosine],
        axis=-1,
    )


def masked_scores(queries, key_rows, allowed, score_scale):
    scores = (
        jnp.einsum("qhd,khd->hqk", queries, key_rows, preferred_element_type=jnp.float32)
        * score_scale
    )
    return jnp.where(allowed[None], scores, -1e30)


def norm_back(grad_normed, source, inv_scale, gain_vec):
    unit_rows = source * inv_scale
    grad_unit = grad_normed * gain_vec
    grad_gain = jnp.sum(grad_normed * unit_rows, axis=0)
    grad_source = inv_scale * (
        grad_unit - unit_rows * jnp.mean(grad_unit * unit_rows, axis=-1, keepdims=True)
    )
    return (grad_source, grad_gain)


def swish_back(pre_gate, pre_up, grad_act):
    sigmoid_vals = jax.nn.sigmoid(pre_gate)
    grad_gate = grad_act * pre_up * sigmoid_vals * (1.0 + pre_gate * (1.0 - sigmoid_vals))
    grad_up = grad_act * pre_gate * sigmoid_vals
    return jnp.stack([grad_gate, grad_up]).astype(jnp.bfloat16)


def body(
    tokens,
    cotangent,
    segments,
    routes,
    gate_weight,
    gain_attn,
    w_qkv,
    b_qkv,
    w_out,
    gain_ffn,
    w_sgu,
    w_sd,
    shared_gate,
    w_egu,
    w_ed,
):
    micro_count = tokens.shape[0]
    token_rows = tokens.shape[1]
    width = tokens.shape[2]
    length = token_rows * lax.axis_size("shard")
    local_experts = w_egu.shape[0]
    expert_total = local_experts * lax.axis_size("expert")
    sources = lax.axis_size("expert")
    capacity = 3 * token_rows * TOP // (2 * expert_total)
    heads_local = b_qkv.shape[1]
    score_scale = HD ** (-0.5)
    vectors = jnp.stack([gain_attn, gain_ffn, shared_gate])
    cosine, sine = rope_tables(length)
    position = jnp.arange(length)
    causal = position[:, None] >= position[None, :]
    expert_ids = jnp.arange(expert_total)
    choice_ids = jnp.arange(token_rows * TOP)
    acc_qkv = jnp.zeros((3, width, w_qkv.shape[2]), jnp.float32)
    acc_bias = jnp.zeros((3, heads_local, HD), jnp.float32)
    acc_out = jnp.zeros((w_out.shape[0], width), jnp.float32)
    acc_sgu = jnp.zeros((2, width, w_sgu.shape[2]), jnp.float32)
    acc_sd = jnp.zeros((w_sd.shape[0], width), jnp.float32)
    acc_vec = jnp.zeros((3, width), jnp.float32)
    acc_egu = jnp.zeros((local_experts, 2, width, FF), jnp.float32)
    acc_ed = jnp.zeros((local_experts, FF, width), jnp.float32)
    mixed_list = []
    grad_rows_list = []
    grad_gate_list = []
    for micro_step in range(micro_count):
        fetched = fetch_weights(vectors, w_qkv, b_qkv, w_out, w_sgu, w_sd, w_egu, w_ed)
        qkv_full, bias_full, out_full, sgu_full, sd_full, vec_full, egu_full, ed_full = fetched
        gain_one = vec_full[0].astype(jnp.float32)
        gain_two = vec_full[1].astype(jnp.float32)
        gate_vec = vec_full[2].astype(jnp.float32)
        source = tokens[micro_step].astype(jnp.float32)
        labels = segments[micro_step, 0]
        scale_one = lax.rsqrt(jnp.mean(source * source, axis=-1, keepdims=True) + EPSILON)
        normed_one = (source * scale_one * gain_one).astype(jnp.bfloat16)
        rows_one = spread_rows(normed_one)
        projected = jnp.einsum(
            "ld,ide->ile", rows_one, qkv_full, preferred_element_type=jnp.float32
        ) + bias_full.reshape(3, 1, -1).astype(jnp.float32)
        split_heads = projected.reshape(3, length, heads_local, HD)
        queries = rotate(split_heads[0], cosine, sine).astype(jnp.bfloat16)
        key_rows = rotate(split_heads[1], cosine, sine).astype(jnp.bfloat16)
        values = split_heads[2].astype(jnp.bfloat16)
        allowed = (labels[:, None] == labels[None, :]) & causal
        scores = masked_scores(queries, key_rows, allowed, score_scale)
        peak_val = jnp.max(scores, axis=-1, keepdims=True)
        expo_vals = jnp.exp(scores - peak_val)
        totals = jnp.sum(expo_vals, axis=-1, keepdims=True)
        log_total = peak_val + jnp.log(totals)
        probabilities = (expo_vals / totals).astype(jnp.bfloat16)
        context = (
            jnp.einsum("hqk,khd->qhd", probabilities, values, preferred_element_type=jnp.float32)
            .reshape(length, -1)
            .astype(jnp.bfloat16)
        )
        attention = fold_rows(jnp.dot(context, out_full, preferred_element_type=jnp.float32))
        hidden = source + attention
        scale_two = lax.rsqrt(jnp.mean(hidden * hidden, axis=-1, keepdims=True) + EPSILON)
        normed_two = (hidden * scale_two * gain_two).astype(jnp.bfloat16)
        rows_two = spread_rows(normed_two)
        shared_in = jnp.einsum(
            "ld,idf->ilf", rows_two, sgu_full, preferred_element_type=jnp.float32
        )
        shared_act = (jax.nn.silu(shared_in[0]) * shared_in[1]).astype(jnp.bfloat16)
        shared_sum = fold_rows(jnp.dot(shared_act, sd_full, preferred_element_type=jnp.float32))
        normed_float = normed_two.astype(jnp.float32)
        opening = jax.nn.sigmoid(jnp.sum(normed_float * gate_vec, axis=-1))
        route_flat = routes[micro_step].reshape(-1)
        one_hot = (route_flat[:, None] == expert_ids[None, :]).astype(jnp.int32)
        slot_rank = jnp.sum((jnp.cumsum(one_hot, axis=0) - 1) * one_hot, axis=1)
        target = route_flat * capacity + slot_rank
        slot_choice = jnp.zeros((expert_total * capacity,), jnp.int32).at[target].set(choice_ids)
        slot_used = jnp.zeros((expert_total * capacity,), jnp.int32).at[target].set(1)
        used_mask = slot_used.astype(jnp.bfloat16)[:, None]
        outgoing = jnp.take(normed_two, slot_choice // TOP, axis=0) * used_mask
        received = trade_rows(outgoing).reshape(sources, local_experts, capacity, width)
        expert_in = jnp.einsum(
            "sjcd,jidf->isjcf", received, egu_full, preferred_element_type=jnp.float32
        )
        expert_act = (jax.nn.silu(expert_in[0]) * expert_in[1]).astype(jnp.bfloat16)
        expert_out = jnp.einsum(
            "sjcf,jfd->sjcd", expert_act, ed_full, preferred_element_type=jnp.float32
        ).astype(jnp.bfloat16)
        returned = trade_rows(expert_out.reshape(-1, width))
        picked_rows = (
            jnp.take(returned, target, axis=0).reshape(token_rows, TOP, width).astype(jnp.float32)
        )
        gates_now = gate_weight[micro_step]
        expert_mix = jnp.einsum("tk,tkd->td", gates_now, picked_rows)
        mixed_list.append(hidden + opening[:, None] * shared_sum + expert_mix)
        grad_out = cotangent[micro_step].astype(jnp.float32)
        grad_gate_list.append(jnp.einsum("tkd,td->tk", picked_rows, grad_out))
        grad_choice = (
            (gates_now[:, :, None] * grad_out[:, None, :]).reshape(-1, width).astype(jnp.bfloat16)
        )
        grad_slots = jnp.take(grad_choice, slot_choice, axis=0) * used_mask
        grad_expert_out = trade_rows(grad_slots).reshape(sources, local_experts, capacity, width)
        grad_expert_act = jnp.einsum(
            "sjcd,jfd->sjcf", grad_expert_out, ed_full, preferred_element_type=jnp.float32
        )
        acc_ed = acc_ed + jnp.einsum(
            "sjcf,sjcd->jfd", expert_act, grad_expert_out, preferred_element_type=jnp.float32
        )
        grad_expert_in = swish_back(expert_in[0], expert_in[1], grad_expert_act)
        grad_received = jnp.einsum(
            "isjcf,jidf->sjcd", grad_expert_in, egu_full, preferred_element_type=jnp.float32
        ).astype(jnp.bfloat16)
        acc_egu = acc_egu + jnp.einsum(
            "sjcd,isjcf->jidf", received, grad_expert_in, preferred_element_type=jnp.float32
        )
        grad_returned = trade_rows(grad_received.reshape(-1, width))
        grad_from_experts = jnp.sum(
            jnp.take(grad_returned, target, axis=0)
            .reshape(token_rows, TOP, width)
            .astype(jnp.float32),
            axis=1,
        )
        grad_shared_sum = (opening[:, None] * grad_out).astype(jnp.bfloat16)
        grad_shared_rows = spread_rows(grad_shared_sum)
        grad_shared_act = jnp.einsum(
            "ld,fd->lf", grad_shared_rows, sd_full, preferred_element_type=jnp.float32
        )
        acc_sd = acc_sd + jnp.einsum(
            "lf,ld->fd", shared_act, grad_shared_rows, preferred_element_type=jnp.float32
        )
        grad_shared_in = swish_back(shared_in[0], shared_in[1], grad_shared_act)
        acc_sgu = acc_sgu + jnp.einsum(
            "ld,ilf->idf", rows_two, grad_shared_in, preferred_element_type=jnp.float32
        )
        grad_from_shared = fold_rows(
            jnp.einsum("ilf,idf->ld", grad_shared_in, sgu_full, preferred_element_type=jnp.float32)
        )
        grad_opening = jnp.sum(grad_out * shared_sum, axis=-1)
        grad_logit = grad_opening * opening * (1.0 - opening)
        grad_gate_vec = jnp.sum(grad_logit[:, None] * normed_float, axis=0)
        grad_normed_two = grad_from_experts + grad_from_shared + grad_logit[:, None] * gate_vec
        grad_hidden_norm, grad_gain_two = norm_back(grad_normed_two, hidden, scale_two, gain_two)
        grad_hidden = grad_out + grad_hidden_norm
        grad_attn_rows = spread_rows(grad_hidden.astype(jnp.bfloat16))
        grad_context = jnp.einsum(
            "ld,ed->le", grad_attn_rows, out_full, preferred_element_type=jnp.float32
        ).astype(jnp.bfloat16)
        acc_out = acc_out + jnp.einsum(
            "le,ld->ed", context, grad_attn_rows, preferred_element_type=jnp.float32
        )
        grad_context_heads = grad_context.reshape(length, heads_local, HD)
        scores_again = masked_scores(queries, key_rows, allowed, score_scale)
        probs_again = jnp.exp(scores_again - log_total)
        grad_probs = jnp.einsum(
            "qhd,khd->hqk", grad_context_heads, values, preferred_element_type=jnp.float32
        )
        row_delta = jnp.sum(probs_again * grad_probs, axis=-1, keepdims=True)
        grad_scores = (probs_again * (grad_probs - row_delta)).astype(jnp.bfloat16)
        grad_values = jnp.einsum(
            "hqk,qhd->khd",
            probs_again.astype(jnp.bfloat16),
            grad_context_heads,
            preferred_element_type=jnp.float32,
        )
        grad_queries = (
            jnp.einsum("hqk,khd->qhd", grad_scores, key_rows, preferred_element_type=jnp.float32)
            * score_scale
        )
        grad_keys = (
            jnp.einsum("hqk,qhd->khd", grad_scores, queries, preferred_element_type=jnp.float32)
            * score_scale
        )
        grad_projected = (
            jnp.stack(
                [rotate(grad_queries, cosine, -sine), rotate(grad_keys, cosine, -sine), grad_values]
            )
            .reshape(3, length, -1)
            .astype(jnp.bfloat16)
        )
        acc_bias = acc_bias + jnp.sum(grad_projected.astype(jnp.float32), axis=1).reshape(
            3, heads_local, HD
        )
        acc_qkv = acc_qkv + jnp.einsum(
            "ld,ile->ide", rows_one, grad_projected, preferred_element_type=jnp.float32
        )
        grad_normed_one = fold_rows(
            jnp.einsum("ile,ide->ld", grad_projected, qkv_full, preferred_element_type=jnp.float32)
        )
        grad_source_norm, grad_gain_one = norm_back(grad_normed_one, source, scale_one, gain_one)
        grad_rows_list.append(grad_hidden + grad_source_norm)
        acc_vec = acc_vec + jnp.stack([grad_gain_one, grad_gain_two, grad_gate_vec])
    summed_qkv, summed_bias, summed_out, summed_sgu, summed_sd, summed_vec = (
        lax.psum_scatter(acc_qkv, "expert", scatter_dimension=1, tiled=True),
        lax.psum_scatter(acc_bias, "expert", scatter_dimension=2, tiled=True),
        lax.psum_scatter(acc_out, "expert", scatter_dimension=1, tiled=True),
        lax.psum_scatter(acc_sgu, "expert", scatter_dimension=1, tiled=True),
        lax.psum_scatter(acc_sd, "expert", scatter_dimension=1, tiled=True),
        lax.psum_scatter(acc_vec, "expert", scatter_dimension=1, tiled=True),
    )
    summed_egu, summed_ed, final_vec = (
        lax.psum_scatter(acc_egu, "shard", scatter_dimension=2, tiled=True),
        lax.psum_scatter(acc_ed, "shard", scatter_dimension=1, tiled=True),
        lax.psum_scatter(summed_vec, "shard", scatter_dimension=1, tiled=True),
    )
    return (
        jnp.stack(mixed_list),
        jnp.stack(grad_rows_list),
        jnp.stack(grad_gate_list),
        final_vec[0],
        summed_qkv,
        summed_bias,
        summed_out,
        final_vec[1],
        summed_sgu,
        summed_sd,
        final_vec[2],
        summed_egu,
        summed_ed,
    )


def solution(mesh):
    return jax.shard_map(
        body,
        mesh=mesh,
        in_specs=(
            P(None, ("expert", "shard"), None),
            P(None, ("expert", "shard"), None),
            P(None, "expert", None),
            P(None, ("expert", "shard"), None),
            P(None, ("expert", "shard"), None),
            P(("expert", "shard")),
            P(None, "expert", "shard"),
            P(None, "shard", "expert"),
            P("shard", "expert"),
            P(("expert", "shard")),
            P(None, "expert", "shard"),
            P("shard", "expert"),
            P(("expert", "shard")),
            P("expert", None, "shard", None),
            P("expert", "shard", None),
        ),
        out_specs=(
            P(None, ("expert", "shard"), None),
            P(None, ("expert", "shard"), None),
            P(None, ("expert", "shard"), None),
            P(("expert", "shard")),
            P(None, "expert", "shard"),
            P(None, "shard", "expert"),
            P("shard", "expert"),
            P(("expert", "shard")),
            P(None, "expert", "shard"),
            P("shard", "expert"),
            P(("expert", "shard")),
            P("expert", None, "shard", None),
            P("expert", "shard", None),
        ),
        check_vma=False,
    )
```

profile of v0, /device:TPU:0, one launch (start us, length us, event | category | flops | bytes accessed | tf_op | source)
XLA Modules:
  0.0 2401.2 jit_solution(1356309962609851512)
XLA Ops:
  15.4 26.9 %all_gather.61 = bf16[3,2048]{1,0:T(4,128)(2,1)S(1)} all-gather(bf16[3,256]{1,0:T(4,128)(2,1)S(1)} %bitcast.596), channel_id=1, replica_groups=mesh['expert'=8,'shard'=4] {'expert'}, dimensions={1}, use_global_device_ids=true | all-gather | bytes 13824 | tf_op jit(solution)/shard_map/all_gather | solution.py:39
  47.3 30.7 %all_gather.64 = bf16[3,4,128]{1,0,2:T(4,128)(2,1)S(1)} all-gather(bf16[3,4,16]{1,0,2:T(4,128)(2,1)S(1)} %copy.261), channel_id=1, replica_groups=mesh['expert'=8,'shard'=4] {'expert'}, dimensions={2}, use_global_device_ids=true | all-gather | bytes 3456 | tf_op jit(solution)/shard_map/all_gather | solution.py:35
  79.4 82.8 %all-gather.18.cloned.1.call-done = bf16[3,2048,512]{2,1,0:T(8,128)(2,1)} async-done(((bf16[3,256,512]{2,1,0:T(8,128)(2,1)}), bf16[3,2048,512]{2,1,0:T(8,128)(2,1)}) %all-gather.18.cloned.1.call-update) | async-done | bytes 6291472 | tf_op jit(solution)/shard_map/all_gather | solution.py:34
  190.3 41.2 %all-gather.20.cloned.1.call-done = bf16[512,2048]{1,0:T(8,128)(2,1)} async-done(((bf16[512,256]{1,0:T(8,128)(2,1)}), bf16[512,2048]{1,0:T(8,128)(2,1)}) %all-gather.20.cloned.1.call-update) | async-done | bytes 2097168 | tf_op jit(solution)/shard_map/all_gather | solution.py:36
  241.3 23.4 reduce-scatter.24.cloned.1.call-done
  264.7 34.2 %reduce-scatter.28.cloned.1.call-done = f32[64,2048]{1,0:T(8,128)} async-done(((f32[256,2048]{1,0:T(8,128)}), f32[64,2048]{1,0:T(8,128)}) %reduce-scatter.28.cloned.1.call-update) | async-done | bytes 524304 | tf_op jit(solution)/shard_map/reduce_scatter | solution.py:20
  305.6 13.5 all-gather.34.cloned.1.call-done
  319.2 165.5 %all-gather.24.cloned.1.call-done = bf16[2,2048,1408]{2,1,0:T(8,128)(2,1)} async-done(((bf16[2,256,1408]{2,1,0:T(8,128)(2,1)}), bf16[2,2048,1408]{2,1,0:T(8,128)(2,1)}) %all-gather.24.cloned.1.call-update) | async-done | bytes 11534352 | tf_op jit(solution)/shard_map/all_gather | solution.py:37
  493.2 84.9 %all-gather.26.cloned.1.call-done = bf16[1408,2048]{1,0:T(8,128)(2,1)} async-done(((bf16[1408,256]{1,0:T(8,128)(2,1)}), bf16[1408,2048]{1,0:T(8,128)(2,1)}) %all-gather.26.cloned.1.call-update) | async-done | bytes 5767184 | tf_op jit(solution)/shard_map/all_gather | solution.py:38
  635.3 36.7 %all-to-all-done = bf16[8,48,2048]{2,1,0:T(8,128)(2,1)S(1)} async-done(((bf16[8,48,2048]{2,1,0:T(8,128)(2,1)}), bf16[8,48,2048]{2,1,0:T(8,128)(2,1)S(1)}, u32[]{:S(2)}, u32[]{:S(2)}) %all-to-all-start) | async-done | bytes 1572896 | tf_op jit(solution)/shard_map/all_to_all | solution.py:24
  697.3 15.7 all-to-all-done.4
  713.0 40.7 %all_to_all.72 = bf16[8,48,2048]{2,1,0:T(8,128)(2,1)} all-to-all(bf16[8,48,2048]{2,1,0:T(8,128)(2,1)S(1)} %bitcast.554), channel_id=1, replica_groups=mesh['expert'=8,'shard'=4] {'expert'}, dimensions={0} | all-to-all | bytes 3145728 | tf_op jit(solution)/shard_map/all_to_all | solution.py:24
  757.6 11.5 fusion.21
  771.6 13.8 all-gather.30.cloned.1.call-done
  860.5 13.0 bitcast_convert_fusion.1
  907.3 12.8 all-to-all-done.5
  944.1 17.0 all-to-all-done.1
  986.8 13.9 all-gather.38.cloned.1.call-done
  1008.1 11.4 all-gather.42.cloned.1.call-done
  1045.8 22.8 reduce-scatter.34.cloned.1.call-done
  1068.6 34.3 %reduce-scatter.38.cloned.1.call-done = f32[64,2048]{1,0:T(8,128)} async-done(((f32[256,2048]{1,0:T(8,128)}), f32[64,2048]{1,0:T(8,128)}) %reduce-scatter.38.cloned.1.call-update) | async-done | bytes 524304 | tf_op jit(solution)/shard_map/reduce_scatter | solution.py:20
  1114.4 56.8 %reduce-scatter.52.cloned.1.call-done = f32[256,3]{1,0:T(8,128)} async-done(((f32[2048,3]{1,0:T(8,128)}), f32[256,3]{1,0:T(8,128)}) %reduce-scatter.52.cloned.1.call-update) | async-done | bytes 3088
  1171.3 11.4 add_bitcast_fusion.1
  1184.0 12.5 fusion.75
  1196.5 15.5 fusion
  1223.0 14.8 add_bitcast_fusion
  1284.2 184.7 %reduce-scatter.40.cloned.1.call-done = f32[3,256,512]{1,2,0:T(8,128)} async-done(((f32[3,2048,512]{1,2,0:T(8,128)}), f32[3,256,512]{1,2,0:T(8,128)}) %reduce-scatter.40.cloned.1.call-update) | async-done | bytes 1572880 | tf_op jit(solution)/shard_map/reduce_scatter | solution.py:292
  1471.9 161.6 %reduce-scatter.48.cloned.1.call-done = f32[1,2,512,1408]{2,3,1,0:T(8,128)} async-done(((f32[1,2,2048,1408]{2,3,1,0:T(8,128)}), f32[1,2,512,1408]{2,3,1,0:T(8,128)}) %reduce-scatter.48.cloned.1.call-update) | async-done | bytes 5767184 | tf_op jit(solution)/shard_map/reduce_scatter | solution.py:300
  1639.7 371.1 %reduce-scatter.44.cloned.1.call-done = f32[2,256,1408]{1,2,0:T(8,128)} async-done(((f32[2,2048,1408]{1,2,0:T(8,128)}), f32[2,256,1408]{1,2,0:T(8,128)}) %reduce-scatter.44.cloned.1.call-update) | async-done | bytes 2883600 | tf_op jit(solution)/shard_map/reduce_scatter | solution.py:295
  2014.2 88.7 %reduce-scatter.42.cloned.1.call-done = f32[512,256]{1,0:T(8,128)} async-done(((f32[512,2048]{1,0:T(8,128)}), f32[512,256]{1,0:T(8,128)}) %reduce-scatter.42.cloned.1.call-update) | async-done | bytes 524304 | tf_op jit(solution)/shard_map/reduce_scatter | solution.py:294
  2102.9 93.6 %reduce-scatter.50.cloned.1.call-done = f32[1,352,2048]{2,1,0:T(8,128)} async-done(((f32[1,1408,2048]{2,1,0:T(8,128)}), f32[1,352,2048]{2,1,0:T(8,128)}) %reduce-scatter.50.cloned.1.call-update) | async-done | bytes 2883600 | tf_op jit(solution)/shard_map/reduce_scatter | solution.py:301
  2196.5 197.5 %reduce-scatter.46.cloned.1.call-done = f32[1408,256]{1,0:T(8,128)} async-done(((f32[1408,2048]{1,0:T(8,128)}), f32[1408,256]{1,0:T(8,128)}) %reduce-scatter.46.cloned.1.call-update) | async-done | bytes 1441808 | tf_op jit(solution)/shard_map/reduce_scatter | solution.py:296
  (599 shorter events, 429.3 us)
Async XLA Ops:
  7.2 72.2 %all-gather.16.cloned.1.call-start = ((), (), s32[]{:S(2)}) async-start(), calls=%async_computation.25 | async-start | bytes 1310720 | tf_op jit(solution)/shard_map/all_gather | solution.py:16
  44.9 117.3 %all-gather.18.cloned.1.call-start = ((), (), s32[]{:S(2)}) async-start(), calls=%async_computation.26 | async-start | bytes 7077888 | tf_op jit(solution)/shard_map/all_gather | solution.py:34
  45.7 133.6 %all-gather.32.cloned.1.call-start = ((), (), s32[]{:S(2)}) async-start(), calls=%async_computation.35 | async-start | bytes 1310720 | tf_op jit(solution)/shard_map/all_gather | solution.py:16
  46.4 185.1 %all-gather.20.cloned.1.call-start = ((), (), s32[]{:S(2)}) async-start(), calls=%async_computation.27 | async-start | bytes 2359296 | tf_op jit(solution)/shard_map/all_gather | solution.py:36
  47.0 217.7 %reduce-scatter.24.cloned.1.call-start = ((), (), s32[]{:S(2)}) async-start(), calls=%async_computation.28 | async-start | bytes 2621440 | tf_op jit(solution)/shard_map/reduce_scatter | solution.py:20
  235.2 63.7 %reduce-scatter.28.cloned.1.call-start = ((), (), s32[]{:S(2)}) async-start(), calls=%async_computation.36 | async-start | bytes 2621440 | tf_op jit(solution)/shard_map/reduce_scatter | solution.py:20
  241.2 77.9 %all-gather.34.cloned.1.call-start = ((), (), s32[]{:S(2)}) async-start(), calls=%async_computation.37 | async-start | bytes 1310720 | tf_op jit(solution)/shard_map/all_gather | solution.py:16
  302.3 182.4 %all-gather.24.cloned.1.call-start = ((), (), s32[]{:S(2)}) async-start(), calls=%async_computation.30 | async-start | bytes 12976128 | tf_op jit(solution)/shard_map/all_gather | solution.py:37
  303.0 275.0 %all-gather.26.cloned.1.call-start = ((), (), s32[]{:S(2)}) async-start(), calls=%async_computation.31 | async-start | bytes 6488064 | tf_op jit(solution)/shard_map/all_gather | solution.py:38
  303.8 291.2 %all-gather.22.cloned.1.call-start = ((), (), s32[]{:S(2)}) async-start(), calls=%async_computation.29 | async-start | bytes 1310720 | tf_op jit(solution)/shard_map/all_gather | solution.py:16
  304.4 453.2 %all-gather.28.cloned.1.call-start = ((), (), s32[]{:S(2)}) async-start(), calls=%async_computation.33 | async-start | bytes 14417920 | tf_op jit(solution)/shard_map/all_gather | solution.py:29
  305.1 463.9 %reduce-scatter.30.cloned.1.call-start = ((), (), s32[]{:S(2)}) async-start(), calls=%async_computation.38 | async-start | bytes 2621440 | tf_op jit(solution)/shard_map/reduce_scatter | solution.py:20
  583.9 185.2 %reduce-scatter.26.cloned.1.call-start = ((), (), s32[]{:S(2)}) async-start(), calls=%async_computation.32 | async-start | bytes 2621440 | tf_op jit(solution)/shard_map/reduce_scatter | solution.py:20
  629.2 42.9 %all-to-all-start = ((bf16[8,48,2048]{2,1,0:T(8,128)(2,1)}), bf16[8,48,2048]{2,1,0:T(8,128)(2,1)S(1)}, u32[]{:S(2)}, u32[]{:S(2)}) async-start(bf16[8,48,2048]{2,1,0:T(8,128)(2,1)} %bitcast.24), calls=%async_computation.2 | async-start | bytes 3145728 | tf_op jit(solution)/shard_map/all_to_all | solution.py:24
  634.7 150.6 %all-gather.30.cloned.1.call-start = ((), (), s32[]{:S(2)}) async-start(), calls=%async_computation.34 | async-start | bytes 7208960 | tf_op jit(solution)/shard_map/all_gather | solution.py:30
  757.3 62.5 %all-gather.36.cloned.1.call-start = ((), (), s32[]{:S(2)}) async-start(), calls=%async_computation.39 | async-start | bytes 1310720 | tf_op jit(solution)/shard_map/all_gather | solution.py:16
  795.2 42.1 %all-to-all-start.3 = ((bf16[8,48,2048]{2,1,0:T(8,128)(2,1)}), bf16[8,48,2048]{2,1,0:T(8,128)(2,1)S(1)}, u32[]{:S(2)}, u32[]{:S(2)}) async-start(bf16[8,48,2048]{2,1,0:T(8,128)(2,1)} %fusion.37), calls=%async_computation.7 | async-start | bytes 3145728 | tf_op jit(solution)/shard_map/all_to_all | solution.py:24
  799.9 83.8 %all-gather.40.cloned.1.call-start = ((), (), s32[]{:S(2)}) async-start(), calls=%async_computation.43 | async-start | bytes 1310720 | tf_op jit(solution)/shard_map/all_gather | solution.py:16
  808.8 172.7 %reduce-scatter.32.cloned.1.call-start = ((), (), s32[]{:S(2)}) async-start(), calls=%async_computation.40 | async-start | bytes 2621440 | tf_op jit(solution)/shard_map/reduce_scatter | solution.py:20
  883.5 98.0 %reduce-scatter.36.cloned.1.call-start = ((), (), s32[]{:S(2)}) async-start(), calls=%async_computation.44 | async-start | bytes 2621440 | tf_op jit(solution)/shard_map/reduce_scatter | solution.py:20
  924.4 76.3 %all-gather.38.cloned.1.call-start = ((), (), s32[]{:S(2)}) async-start(), calls=%async_computation.41 | async-start | bytes 1310720 | tf_op jit(solution)/shard_map/all_gather | solution.py:16
  986.4 82.2 %reduce-scatter.34.cloned.1.call-start = ((), (), s32[]{:S(2)}) async-start(), calls=%async_computation.42 | async-start | bytes 2621440 | tf_op jit(solution)/shard_map/reduce_scatter | solution.py:20
  1037.3 65.6 %reduce-scatter.38.cloned.1.call-start = ((), (), s32[]{:S(2)}) async-start(), calls=%async_computation.46 | async-start | bytes 2621440 | tf_op jit(solution)/shard_map/reduce_scatter | solution.py:20
  1045.6 125.5 %reduce-scatter.52.cloned.1.call-start = ((), (), s32[]{:S(2)}) async-start(), calls=%async_computation.53 | async-start | bytes 1179648
  1106.6 169.0 %reduce-scatter.56.cloned.1.call-start = ((), (), s32[]{:S(2)}) async-start(), calls=%async_computation.55 | async-start | bytes 73728
  1107.8 173.8 %reduce-scatter.54.cloned.1.call-start = ((), (), s32[]{:S(2)}) async-start(), calls=%async_computation.54 | async-start | bytes 163840
  1171.2 297.7 %reduce-scatter.40.cloned.1.call-start = ((), (), s32[]{:S(2)}) async-start(), calls=%async_computation.47 | async-start | bytes 14155776 | tf_op jit(solution)/shard_map/reduce_scatter | solution.py:292
  1182.6 450.9 %reduce-scatter.48.cloned.1.call-start = ((), (), s32[]{:S(2)}) async-start(), calls=%async_computation.51 | async-start | bytes 28835840 | tf_op jit(solution)/shard_map/reduce_scatter | solution.py:300
  1212.0 798.8 %reduce-scatter.44.cloned.1.call-start = ((), (), s32[]{:S(2)}) async-start(), calls=%async_computation.49 | async-start | bytes 25952256 | tf_op jit(solution)/shard_map/reduce_scatter | solution.py:295
  1237.9 865.1 %reduce-scatter.42.cloned.1.call-start = ((), (), s32[]{:S(2)}) async-start(), calls=%async_computation.48 | async-start | bytes 4718592 | tf_op jit(solution)/shard_map/reduce_scatter | solution.py:294
  1242.7 953.8 %reduce-scatter.50.cloned.1.call-start = ((), (), s32[]{:S(2)}) async-start(), calls=%async_computation.52 | async-start | bytes 14417920 | tf_op jit(solution)/shard_map/reduce_scatter | solution.py:301
  1257.3 1136.7 %reduce-scatter.46.cloned.1.call-start = ((), (), s32[]{:S(2)}) async-start(), calls=%async_computation.50 | async-start | bytes 12976128 | tf_op jit(solution)/shard_map/reduce_scatter | solution.py:296
  (153 other events, 2293.8 us)
Sparse Core Ops, SparseCore 0:
  45.1 16.1 all-gather.15
  63.4 98.7 all-gather.17
  164.3 14.8 all-gather.31
  181.2 50.3 all-gather.19
  235.3 29.3 reduce-scatter.23
  267.7 31.1 reduce-scatter.27
  302.4 16.6 all-gather.33
  321.3 163.2 all-gather.23
  486.7 91.3 all-gather.25
  580.1 14.8 all-gather.21
  596.6 76.1 all-gather.27
  675.1 31.1 reduce-scatter.29
  709.4 31.1 reduce-scatter.25
  742.0 43.3 all-gather.29
  787.4 16.6 all-gather.35
  808.9 17.1 all-gather.39
  835.9 31.5 reduce-scatter.31
  899.7 31.5 reduce-scatter.35
  985.9 14.7 all-gather.37
  1002.7 16.6 all-gather.41
  1037.4 31.1 reduce-scatter.33
  1071.7 31.1 reduce-scatter.37
  1106.9 64.2 reduce-scatter.51
  1175.0 61.3 reduce-scatter.55
  1238.8 18.6 reduce-scatter.53
  1261.0 207.9 reduce-scatter.39
  1471.4 162.0 reduce-scatter.47
  1637.4 373.3 reduce-scatter.43
  2015.0 87.8 reduce-scatter.41
  2105.9 90.5 reduce-scatter.49
  2200.7 193.2 reduce-scatter.45
where the time goes:
time: 2410 us; the launch traced here: 2400 us
  waiting for transfers between devices  1810 us (75%)
  matrix products  275 us (11%)
  local copies, waits for them, and re-layouts  106 us (4%)
  blocking collectives  104 us (4%)
  other arithmetic  54.4 us (2%)
  starting transfers between devices  35.1 us (1%)
    reduce_scatter x1, waiting for transfers between devices, body(): lax.psum_scatter(acc_sgu, 'expert', scatter_dimension=1, tiled=True)  371 us
    reduce_scatter x1, waiting for transfers between devices, body(): lax.psum_scatter(acc_sd, 'expert', scatter_dimension=1, tiled=True)  197 us
    reduce_scatter x1, waiting for transfers between devices, body(): lax.psum_scatter(acc_qkv, 'expert', scatter_dimension=1, tiled=True)  185 us
    all_gather x1, waiting for transfers between devices, fetch_weights(): lax.all_gather(w_sgu, 'expert', axis=1, tiled=True)  166 us
    reduce_scatter x1, waiting for transfers between devices, body(): lax.psum_scatter(acc_egu, 'shard', scatter_dimension=2, tiled=True)  162 us
    reduce_scatter x8, waiting for transfers between devices, fold_rows(): return lax.psum_scatter(payload, 'shard', scatter_dimension=0, tiled=True)  115 us
    reduce_scatter x1, waiting for transfers between devices, body(): lax.psum_scatter(acc_ed, 'shard', scatter_dimension=1, tiled=True)  93.6 us
    all_to_all x7, waiting for transfers between devices, trade_rows(): lax.all_to_all(payload, 'expert', split_axis=0, concat_axis=0, tiled=True)  90.3 us
  transfers between devices with their start and end apart: 38, of which 28 were waited for; matrix products, arithmetic and copies ran while one was open for 16% of the time, Pallas kernels for 0%

commit v1 on v0

v1 whole, which is shorter than its diff:
```python
import jax
import jax.numpy as jnp
from jax import lax
from jax.sharding import PartitionSpec as P

HD = 128
EPSILON = 1e-06
ROPE_BASE = 1000000.0
F32 = jnp.float32
BF16 = jnp.bfloat16


def dot(spec, left, right):
    return jnp.einsum(spec, left, right, preferred_element_type=F32)


def spread_rows(rows):
    return lax.all_gather(rows, "shard", axis=0, tiled=True)


def fold_rows(rows):
    return lax.psum_scatter(rows.astype(BF16), "shard", scatter_dimension=0, tiled=True).astype(F32)


def spread_experts(rows):
    return lax.all_gather(rows, "expert", axis=0, tiled=True)


def fold_experts(rows):
    return lax.psum_scatter(rows.astype(BF16), "expert", scatter_dimension=0, tiled=True).astype(F32)


def rotate(tensor, cosine, sine):
    half = tensor.shape[-1] // 2
    first, second = tensor[..., :half], tensor[..., half:]
    return jnp.concatenate([first * cosine - second * sine, first * sine + second * cosine], axis=-1)


def norm_back(grad_normed, source, inv_scale, gain):
    unit = source * inv_scale
    grad_unit = grad_normed * gain
    grad_source = inv_scale * (grad_unit - unit * jnp.mean(grad_unit * unit, axis=-1, keepdims=True))
    return grad_source, jnp.sum(grad_normed * unit, axis=0)


def swish_back(gate, up, grad_act):
    sig = jax.nn.sigmoid(gate)
    grad_gate = grad_act * up * sig * (1.0 + gate * (1.0 - sig))
    grad_up = grad_act * gate * sig
    return jnp.stack([grad_gate, grad_up]).astype(BF16)


def body(
    tokens, cotangent, segments, routes, gate_weight, gain_attn, w_qkv, b_qkv, w_out,
    gain_ffn, w_sgu, w_sd, shared_gate, w_egu, w_ed,
):
    micro, span, width = tokens.shape
    shards = lax.axis_size("shard")
    experts = lax.axis_size("expert") * w_egu.shape[0]
    own = w_egu.shape[0]
    count = micro * span
    length = span * shards
    heads = b_qkv.shape[1]
    score_scale = HD ** (-0.5)

    vectors = jnp.stack([gain_attn, gain_ffn, shared_gate])
    vectors = lax.all_gather(vectors, ("expert", "shard"), axis=1, tiled=True)
    bias = lax.all_gather(b_qkv, "expert", axis=2, tiled=True)
    qkv = lax.all_gather(w_qkv, "expert", axis=1, tiled=True)
    out = lax.all_gather(w_out, "expert", axis=1, tiled=True)
    sgu = lax.all_gather(w_sgu, "expert", axis=1, tiled=True)
    sd = lax.all_gather(w_sd, "expert", axis=1, tiled=True)
    egu = lax.all_gather(w_egu, "shard", axis=2, tiled=True)
    ed = lax.all_gather(w_ed, "shard", axis=1, tiled=True)

    gain_one, gain_two, gate_vec = (vectors[i].astype(F32) for i in range(3))
    source = tokens.reshape(count, width).astype(F32)
    grad_low = cotangent.reshape(count, width)
    grad_out = grad_low.astype(F32)
    chosen = (routes.reshape(count, -1)[:, :, None] == jnp.arange(experts)).astype(F32)
    gates = jnp.sum(chosen * gate_weight.reshape(count, -1)[:, :, None], axis=1)
    gates = gates.T.reshape(-1, own, count)
    gates = lax.all_to_all(gates, "expert", split_axis=0, concat_axis=0, tiled=True)
    gates = gates.transpose(1, 0, 2).reshape(own, -1)
    grad_all = spread_experts(grad_low)

    scale_one = lax.rsqrt(jnp.mean(source * source, axis=-1, keepdims=True) + EPSILON)
    normed_one = (source * scale_one * gain_one).astype(BF16)
    rows_one = spread_rows(normed_one)
    projected = dot("ld,ide->ile", rows_one, qkv) + bias.reshape(3, 1, -1).astype(F32)

    place = jnp.arange(length).astype(F32)
    frequency = ROPE_BASE ** (-jnp.arange(HD // 2).astype(F32) * 2.0 / HD)
    angles = place[:, None] * frequency[None, :]
    cosine, sine = jnp.cos(angles), jnp.sin(angles)

    def to_heads(rows):
        grid = rows.reshape(shards, micro, span, heads, HD).transpose(1, 3, 0, 2, 4)
        return grid.reshape(micro, heads, length, HD)

    def to_rows(grid):
        grid = grid.reshape(micro, heads, shards, span, HD).transpose(2, 0, 3, 1, 4)
        return grid.reshape(shards * count, heads * HD)

    queries = rotate(to_heads(projected[0]), cosine, sine).astype(BF16)
    keys = rotate(to_heads(projected[1]), cosine, sine).astype(BF16)
    values = to_heads(projected[2]).astype(BF16)
    labels = segments[:, 0]
    index = jnp.arange(length)
    allowed = (labels[:, :, None] == labels[:, None, :]) & (index[:, None] >= index[None, :])
    allowed = allowed[:, None]
    scores = jnp.where(allowed, dot("mhqd,mhkd->mhqk", queries, keys) * score_scale, -1e30)
    peak = jnp.max(scores, axis=-1, keepdims=True)
    expo = jnp.exp(scores - peak)
    total = jnp.sum(expo, axis=-1, keepdims=True)
    exact = expo / total
    probs = exact.astype(BF16)
    context = to_rows(dot("mhqk,mhkd->mhqd", probs, values).astype(BF16))
    hidden = source + fold_rows(dot("le,ed->ld", context, out))

    scale_two = lax.rsqrt(jnp.mean(hidden * hidden, axis=-1, keepdims=True) + EPSILON)
    normed_two = (hidden * scale_two * gain_two).astype(BF16)
    rows_two = spread_rows(normed_two)
    routed = spread_experts(normed_two)
    shared_in = dot("ld,idf->ilf", rows_two, sgu)
    shared_act = (jax.nn.silu(shared_in[0]) * shared_in[1]).astype(BF16)
    shared_sum = fold_rows(dot("lf,fd->ld", shared_act, sd))
    normed_float = normed_two.astype(F32)
    opening = jax.nn.sigmoid(jnp.sum(normed_float * gate_vec, axis=-1))

    expert_in = dot("rd,jidf->ijrf", routed, egu)
    expert_act = (jax.nn.silu(expert_in[0]) * expert_in[1]).astype(BF16)
    expert_out = dot("jrf,jfd->jrd", expert_act, ed).astype(BF16).astype(F32)
    blend = fold_experts(jnp.sum(gates[:, :, None] * expert_out, axis=0))
    mixed = hidden + opening[:, None] * shared_sum + blend
    grad_all_float = grad_all.astype(F32)
    inner = jnp.sum(expert_out * grad_all_float, axis=-1)
    inner = inner.reshape(own, -1, count).transpose(1, 0, 2)
    inner = lax.all_to_all(inner, "expert", split_axis=0, concat_axis=0, tiled=True)
    inner = inner.reshape(experts, count)
    grad_gate = jnp.sum(chosen * inner.T[:, None, :], axis=-1)

    grad_expert = (gates[:, :, None] * grad_all_float).astype(BF16)
    grad_expert_act = dot("jrd,jfd->jrf", grad_expert, ed)
    grad_ed = dot("jrf,jrd->jfd", expert_act, grad_expert)
    grad_expert_in = swish_back(expert_in[0], expert_in[1], grad_expert_act)
    grad_routed = dot("ijrf,jidf->rd", grad_expert_in, egu)
    grad_egu = dot("rd,ijrf->jidf", routed, grad_expert_in)
    grad_from_experts = fold_experts(grad_routed)

    grad_shared = (opening[:, None] * grad_out).astype(BF16)
    grad_shared_rows = spread_rows(grad_shared)
    grad_shared_act = dot("ld,fd->lf", grad_shared_rows, sd)
    grad_sd = dot("lf,ld->fd", shared_act, grad_shared_rows)
    grad_shared_in = swish_back(shared_in[0], shared_in[1], grad_shared_act)
    grad_sgu = dot("ld,ilf->idf", rows_two, grad_shared_in)
    grad_from_shared = fold_rows(dot("ilf,idf->ld", grad_shared_in, sgu))
    grad_opening = jnp.sum(grad_out * shared_sum, axis=-1)
    grad_logit = grad_opening * opening * (1.0 - opening)
    grad_gate_vec = jnp.sum(grad_logit[:, None] * normed_float, axis=0)
    grad_normed_two = grad_from_experts + grad_from_shared + grad_logit[:, None] * gate_vec
    grad_hidden, grad_gain_two = norm_back(grad_normed_two, hidden, scale_two, gain_two)
    grad_hidden = grad_out + grad_hidden

    grad_rows = spread_rows(grad_hidden.astype(BF16))
    grad_context = to_heads(dot("ld,ed->le", grad_rows, out).astype(BF16))
    grad_out_w = dot("le,ld->ed", context, grad_rows)
    grad_probs = dot("mhqd,mhkd->mhqk", grad_context, values)
    delta = jnp.sum(exact * grad_probs, axis=-1, keepdims=True)
    grad_scores = (exact * (grad_probs - delta)).astype(BF16)
    grad_values = dot("mhqk,mhqd->mhkd", probs, grad_context)
    grad_queries = dot("mhqk,mhkd->mhqd", grad_scores, keys) * score_scale
    grad_keys = dot("mhqk,mhqd->mhkd", grad_scores, queries) * score_scale
    grad_projected = jnp.stack(
        [
            to_rows(rotate(grad_queries, cosine, -sine)),
            to_rows(rotate(grad_keys, cosine, -sine)),
            to_rows(grad_values),
        ]
    ).astype(BF16)
    grad_bias = jnp.sum(grad_projected.astype(F32), axis=1).reshape(3, heads, HD)
    grad_qkv = dot("ld,ile->ide", rows_one, grad_projected)
    grad_normed_one = fold_rows(dot("ile,ide->ld", grad_projected, qkv))
    grad_source, grad_gain_one = norm_back(grad_normed_one, source, scale_one, gain_one)
    grad_tokens = grad_hidden + grad_source

    def fold_weights(value, axis, dim):
        return lax.psum_scatter(value.astype(BF16), axis, scatter_dimension=dim, tiled=True).astype(F32)

    summed_ed = fold_weights(grad_ed, "shard", 1)
    summed_egu = fold_weights(grad_egu, "shard", 2)
    summed_sd = fold_weights(grad_sd, "expert", 1)
    summed_sgu = fold_weights(grad_sgu, "expert", 1)
    summed_out = fold_weights(grad_out_w, "expert", 1)
    summed_qkv = fold_weights(grad_qkv, "expert", 1)
    summed_bias = lax.psum_scatter(grad_bias, "expert", scatter_dimension=2, tiled=True)
    gains = jnp.stack([grad_gain_one, grad_gain_two, grad_gate_vec])
    gains = lax.psum_scatter(gains, ("expert", "shard"), scatter_dimension=1, tiled=True)
    shape = tokens.shape
    return (
        mixed.reshape(shape),
        grad_tokens.reshape(shape),
        grad_gate.reshape(routes.shape),
        gains[0],
        summed_qkv,
        summed_bias,
        summed_out,
        gains[1],
        summed_sgu,
        summed_sd,
        gains[2],
        summed_egu,
        summed_ed,
    )


def solution(mesh):
    both = ("expert", "shard")
    rows = P(None, both, None)
    parameters = (
        P(None, "expert", "shard"),
        P(None, "shard", "expert"),
        P("shard", "expert"),
        P(both),
        P(None, "expert", "shard"),
        P("shard", "expert"),
        P(both),
        P("expert", None, "shard", None),
        P("expert", "shard", None),
    )
    return jax.shard_map(
        body,
        mesh=mesh,
        in_specs=(rows, rows, P(None, "expert", None), rows, rows, P(both)) + parameters,
        out_specs=(rows, rows, rows, P(both)) + parameters,
        check_vma=False,
    )
```

time: 2410 us -> 2050 us (0.85)
  waiting for transfers between devices: 1810 us -> 1670 us
  matrix products: 275 us -> 185 us
  local copies, waits for them, and re-layouts: 106 us -> 49.6 us
  blocking collectives: 104 us -> 74 us
    reduce_scatter x14 -> x12, waiting for transfers between devices: 1210 us -> 816 us  [the longest x6 594 us: fold_weights(): lax.psum_scatter(value.astype(BF16), axis, scatter_dimension=dim, tiled=T...]
    all_gather x14 -> x12, waiting for transfers between devices: 445 us -> 641 us  [the longest x1 165 us: body(): sgu = lax.all_gather(w_sgu, 'expert', axis=1, tiled=True)]
    unnamed x34 -> x28, waiting for transfers between devices: 62.6 us -> 203 us
    dot_general x52 -> x23, matrix products: 275 us -> 182 us  [dot(): return jnp.einsum(spec, left, right, preferred_element_type=F32)]
    all_to_all x7 -> x2, waiting for transfers between devices: 90.3 us -> 6.23 us  [the longest x1 6.23 us: body(): lax.all_to_all(inner, 'expert', split_axis=0, concat_axis=0, tiled=True)]
    all_to_all x1 -> x0, blocking collectives: 40.7 us -> none  [trade_rows(): lax.all_to_all(payload, 'expert', split_axis=0, concat_axis=0, tiled=True)]
    gather x8 -> x0, local copies, waits for them, and re-layouts: 28.8 us -> none  [the longest x2 9.02 us: body(): jnp.take(grad_returned, target, axis=0).reshape(token_rows, TOP, width)]
    all_gather x3 -> x2, blocking collectives: 63.7 us -> 73.9 us  [the longest x1 43.3 us: body(): vectors = lax.all_gather(vectors, ('expert', 'shard'), axis=1, tiled=True)]
  transfers between devices with their start and end apart: 38 -> 28, of which waited for: 28 -> 25; matrix products, arithmetic and copies ran while one was open for 16% -> 11% of each run, Pallas kernels for 0% -> 0%
where the time goes in v1:
time: 2050 us; the launch traced here: 2040 us
  waiting for transfers between devices  1670 us (81%)
  matrix products  185 us (9%)
  blocking collectives  74 us (4%)
  local copies, waits for them, and re-layouts  49.6 us (2%)
  other arithmetic  40.1 us (2%)
    reduce_scatter x6, waiting for transfers between devices, fold_weights(): lax.psum_scatter(value.astype(BF16), axis, scatter_dimension=dim, tiled=T...  594 us
    unnamed x28, waiting for transfers between devices  203 us
    dot_general x23, matrix products, dot(): return jnp.einsum(spec, left, right, preferred_element_type=F32)  182 us
    all_gather x1, waiting for transfers between devices, body(): sgu = lax.all_gather(w_sgu, 'expert', axis=1, tiled=True)  165 us
    reduce_scatter x2, waiting for transfers between devices, fold_experts(): lax.psum_scatter(rows.astype(BF16), 'expert', scatter_dimension=0, tiled=...  153 us
    all_gather x2, waiting for transfers between devices, spread_experts(): return lax.all_gather(rows, 'expert', axis=0, tiled=True)  125 us
    all_gather x1, waiting for transfers between devices, body(): qkv = lax.all_gather(w_qkv, 'expert', axis=1, tiled=True)  85.9 us
    all_gather x1, waiting for transfers between devices, body(): sd = lax.all_gather(w_sd, 'expert', axis=1, tiled=True)  79.8 us
  transfers between devices with their start and end apart: 28, of which 25 were waited for; matrix products, arithmetic and copies ran while one was open for 11% of the time, Pallas kernels for 0%

profile of v1, /device:TPU:0, one launch (start us, length us, event | category | flops | bytes accessed | tf_op | source)
XLA Modules:
  0.0 2041.9 jit_solution(17479774930001592125)
XLA Ops:
  9.3 43.3 %all-gather = bf16[32,64,3]{1,2,0:T(4,128)(2,1)S(1)} all-gather(bf16[1,64,3]{1,2,0:T(4,128)(2,1)S(1)} %maximum_bitcast_fusion), channel_id=1, replica_groups=mesh['expert'=8,'shard'=4] {'expert','shard'}, dimensions={0}, use_global_device_ids=true | all-gather | bytes 12672 | tf_op jit(solution)/shard_map/all_gather | solution.py:67
  56.5 30.6 %all_gather.45 = bf16[3,4,128]{1,0,2:T(4,128)(2,1)S(1)} all-gather(bf16[3,4,16]{1,0,2:T(4,128)(2,1)S(1)} %copy.177), channel_id=1, replica_groups=mesh['expert'=8,'shard'=4] {'expert'}, dimensions={2}, use_global_device_ids=true | all-gather | bytes 3456 | tf_op jit(solution)/shard_map/all_gather | solution.py:68
  88.7 85.9 %all-gather.16.cloned.1.call-done = bf16[3,2048,512]{2,1,0:T(8,128)(2,1)} async-done(((bf16[3,256,512]{2,1,0:T(8,128)(2,1)}), bf16[3,2048,512]{2,1,0:T(8,128)(2,1)}) %all-gather.16.cloned.1.call-update) | async-done | bytes 6291472 | tf_op jit(solution)/shard_map/all_gather | solution.py:69
  192.2 32.9 %all-gather.18.cloned.1.call-done = bf16[512,2048]{1,0:T(8,128)(2,1)} async-done(((bf16[512,256]{1,0:T(8,128)(2,1)}), bf16[512,2048]{1,0:T(8,128)(2,1)}) %all-gather.18.cloned.1.call-update) | async-done | bytes 2097168 | tf_op jit(solution)/shard_map/all_gather | solution.py:70
  229.4 29.5 %reduce-scatter.19.cloned.1.call-done = bf16[128,2048]{1,0:T(8,128)(2,1)} async-done(((bf16[512,2048]{1,0:T(8,128)(2,1)}), bf16[128,2048]{1,0:T(8,128)(2,1)}) %reduce-scatter.19.cloned.1.call-update) | async-done | bytes 524304 | tf_op jit(solution)/shard_map/reduce_scatter | solution.py:22
  266.7 18.4 all-gather.20.cloned.1.call-done
  285.1 165.4 %all-gather.22.cloned.1.call-done = bf16[2,2048,1408]{2,1,0:T(8,128)(2,1)} async-done(((bf16[2,256,1408]{2,1,0:T(8,128)(2,1)}), bf16[2,2048,1408]{2,1,0:T(8,128)(2,1)}) %all-gather.22.cloned.1.call-update) | async-done | bytes 11534352 | tf_op jit(solution)/shard_map/all_gather | solution.py:71
  450.5 10.1 convolution_bitcast_fusion
  464.0 79.8 %all-gather.24.cloned.1.call-done = bf16[1408,2048]{1,0:T(8,128)(2,1)} async-done(((bf16[1408,256]{1,0:T(8,128)(2,1)}), bf16[1408,2048]{1,0:T(8,128)(2,1)}) %all-gather.24.cloned.1.call-update) | async-done | bytes 5767184 | tf_op jit(solution)/shard_map/all_gather | solution.py:72
  551.1 68.7 %all-gather.28.cloned.1.call-done = bf16[1,2,2048,1408]{3,2,1,0:T(8,128)(2,1)} async-done(((bf16[1,2,512,1408]{3,2,1,0:T(8,128)(2,1)}), bf16[1,2,2048,1408]{3,2,1,0:T(8,128)(2,1)}) %all-gather.28.cloned.1.call-update) | async-done | bytes 11534352 | tf_op jit(solution)/shard_map/all_gather | solution.py:73
  619.8 75.5 %all-gather.26.cloned.1.call-done = bf16[1024,2048]{1,0:T(8,128)(2,1)} async-done(((bf16[128,2048]{1,0:T(8,128)(2,1)}), bf16[1024,2048]{1,0:T(8,128)(2,1)}) %all-gather.26.cloned.1.call-update) | async-done | bytes 4194320 | tf_op jit(solution)/shard_map/all_gather | solution.py:26
  695.3 17.2 fusion.3
  719.5 49.2 %all-gather.32.cloned.1.call-done = bf16[1024,2048]{1,0:T(8,128)(2,1)} async-done(((bf16[128,2048]{1,0:T(8,128)(2,1)}), bf16[1024,2048]{1,0:T(8,128)(2,1)}) %all-gather.32.cloned.1.call-update) | async-done | bytes 4194320 | tf_op jit(solution)/shard_map/all_gather | solution.py:26
  768.6 43.5 %all-gather.30.cloned.1.call-done = bf16[1,1408,2048]{2,1,0:T(8,128)(2,1)} async-done(((bf16[1,352,2048]{2,1,0:T(8,128)(2,1)}), bf16[1,1408,2048]{2,1,0:T(8,128)(2,1)}) %all-gather.30.cloned.1.call-update) | async-done | bytes 5767184 | tf_op jit(solution)/shard_map/all_gather | solution.py:74
  812.1 12.2 fusion.7
  848.6 14.3 fusion.33
  865.4 16.3 bitcast_convert_fusion
  907.6 62.6 %reduce-scatter.25.cloned.1.call-done = bf16[128,2048]{1,0:T(8,128)(2,1)} async-done(((bf16[1024,2048]{1,0:T(8,128)(2,1)}), bf16[128,2048]{1,0:T(8,128)(2,1)}) %reduce-scatter.25.cloned.1.call-update) | async-done | bytes 524304 | tf_op jit(solution)/shard_map/reduce_scatter | solution.py:30
  970.2 33.2 %reduce-scatter.27.cloned.1.call-done = bf16[128,2048]{1,0:T(8,128)(2,1)} async-done(((bf16[512,2048]{1,0:T(8,128)(2,1)}), bf16[128,2048]{1,0:T(8,128)(2,1)}) %reduce-scatter.27.cloned.1.call-update) | async-done | bytes 524304 | tf_op jit(solution)/shard_map/reduce_scatter | solution.py:22
  1005.2 90.6 %reduce-scatter.23.cloned.1.call-done = bf16[128,2048]{1,0:T(8,128)(2,1)} async-done(((bf16[1024,2048]{1,0:T(8,128)(2,1)}), bf16[128,2048]{1,0:T(8,128)(2,1)}) %reduce-scatter.23.cloned.1.call-update) | async-done | bytes 524304 | tf_op jit(solution)/shard_map/reduce_scatter | solution.py:30
  1099.5 22.1 %all-gather.36.cloned.1.call-done = bf16[512,2048]{1,0:T(8,128)(2,1)} async-done(((bf16[128,2048]{1,0:T(8,128)(2,1)}), bf16[512,2048]{1,0:T(8,128)(2,1)}) %all-gather.36.cloned.1.call-update) | async-done | bytes 2097168 | tf_op jit(solution)/shard_map/all_gather | solution.py:18
  1145.9 11.1 fusion.8
  1180.1 18.3 convert_bitcast_fusion
  1207.6 10.6 convert_bitcast_fusion.1
  1219.6 14.9 reduce-scatter.41.cloned.1.call-done
  1237.8 62.4 %reduce-scatter.45.cloned.1.call-done = f32[16,12]{1,0:T(8,128)} async-done(((f32[128,12]{1,0:T(8,128)}), f32[16,12]{1,0:T(8,128)}) %reduce-scatter.45.cloned.1.call-update) | async-done | bytes 784
  1301.7 112.9 %reduce-scatter.37.cloned.1.call-done = bf16[1408,256]{1,0:T(8,128)(2,1)} async-done(((bf16[1408,2048]{1,0:T(8,128)(2,1)}), bf16[1408,256]{1,0:T(8,128)(2,1)}) %reduce-scatter.37.cloned.1.call-update) | async-done | bytes 720912 | tf_op jit(solution)/shard_map/reduce_scatter | solution.py:188
  1416.9 69.4 %reduce-scatter.33.cloned.1.call-done = bf16[512,256]{1,0:T(8,128)(2,1)} async-done(((bf16[512,2048]{1,0:T(8,128)(2,1)}), bf16[512,256]{1,0:T(8,128)(2,1)}) %reduce-scatter.33.cloned.1.call-update) | async-done | bytes 262160 | tf_op jit(solution)/shard_map/reduce_scatter | solution.py:188
  1489.5 135.3 %reduce-scatter.43.cloned.1.call-done = f32[64,3]{1,0:T(8,128)} async-done(((f32[2048,3]{1,0:T(8,128)}), f32[64,3]{1,0:T(8,128)}) %reduce-scatter.43.cloned.1.call-update) | async-done | bytes 784
  1627.5 86.4 %reduce-scatter.39.cloned.1.call-done = bf16[1,2,512,1408]{2,3,1,0:T(8,128)(2,1)} async-done(((bf16[1,2,2048,1408]{2,3,1,0:T(8,128)(2,1)}), bf16[1,2,512,1408]{2,3,1,0:T(8,128)(2,1)}) %reduce-scatter.39.cloned.1.call-update) | async-done | bytes 2883600 | tf_op jit(solution)/shard_map/reduce_scatter | solution.py:188
  1719.0 116.9 %reduce-scatter.31.cloned.1.call-done = bf16[3,256,512]{1,2,0:T(8,128)(2,1)} async-done(((bf16[3,2048,512]{1,2,0:T(8,128)(2,1)}), bf16[3,256,512]{1,2,0:T(8,128)(2,1)}) %reduce-scatter.31.cloned.1.call-update) | async-done | bytes 786448 | tf_op jit(solution)/shard_map/reduce_scatter | solution.py:188
  1838.5 193.4 %reduce-scatter.35.cloned.1.call-done = bf16[2,256,1408]{1,2,0:T(8,128)(2,1)} async-done(((bf16[2,2048,1408]{1,2,0:T(8,128)(2,1)}), bf16[2,256,1408]{1,2,0:T(8,128)(2,1)}) %reduce-scatter.35.cloned.1.call-update) | async-done | bytes 1441808 | tf_op jit(solution)/shard_map/reduce_scatter | solution.py:188
  (244 shorter events, 193.7 us)
Async XLA Ops:
  7.2 81.5 %all-gather.14.cloned.1.call-start = ((), (), s32[]{:S(2)}) async-start(), calls=%async_computation.16 | async-start | bytes 2621440 | tf_op jit(solution)/shard_map/all_gather | solution.py:18
  54.8 119.7 %all-gather.16.cloned.1.call-start = ((), (), s32[]{:S(2)}) async-start(), calls=%async_computation.17 | async-start | bytes 7077888 | tf_op jit(solution)/shard_map/all_gather | solution.py:69
  55.6 169.6 %all-gather.18.cloned.1.call-start = ((), (), s32[]{:S(2)}) async-start(), calls=%async_computation.18 | async-start | bytes 2359296 | tf_op jit(solution)/shard_map/all_gather | solution.py:70
  56.3 202.6 %reduce-scatter.19.cloned.1.call-start = ((), (), s32[]{:S(2)}) async-start(), calls=%async_computation.19 | async-start | bytes 2621440 | tf_op jit(solution)/shard_map/reduce_scatter | solution.py:22
  229.4 55.7 %all-gather.20.cloned.1.call-start = ((), (), s32[]{:S(2)}) async-start(), calls=%async_computation.20 | async-start | bytes 2621440 | tf_op jit(solution)/shard_map/all_gather | solution.py:18
  262.4 188.1 %all-gather.22.cloned.1.call-start = ((), (), s32[]{:S(2)}) async-start(), calls=%async_computation.21 | async-start | bytes 12976128 | tf_op jit(solution)/shard_map/all_gather | solution.py:71
  262.9 280.9 %all-gather.24.cloned.1.call-start = ((), (), s32[]{:S(2)}) async-start(), calls=%async_computation.22 | async-start | bytes 6488064 | tf_op jit(solution)/shard_map/all_gather | solution.py:72
  263.7 356.1 %all-gather.28.cloned.1.call-start = ((), (), s32[]{:S(2)}) async-start(), calls=%async_computation.25 | async-start | bytes 14417920 | tf_op jit(solution)/shard_map/all_gather | solution.py:73
  264.4 430.9 %all-gather.26.cloned.1.call-start = ((), (), s32[]{:S(2)}) async-start(), calls=%async_computation.24 | async-start | bytes 4718592 | tf_op jit(solution)/shard_map/all_gather | solution.py:26
  265.2 503.5 %all-gather.32.cloned.1.call-start = ((), (), s32[]{:S(2)}) async-start(), calls=%async_computation.28 | async-start | bytes 4718592 | tf_op jit(solution)/shard_map/all_gather | solution.py:26
  265.8 546.4 %all-gather.30.cloned.1.call-start = ((), (), s32[]{:S(2)}) async-start(), calls=%async_computation.26 | async-start | bytes 7208960 | tf_op jit(solution)/shard_map/all_gather | solution.py:74
  266.5 579.8 %reduce-scatter.21.cloned.1.call-start = ((), (), s32[]{:S(2)}) async-start(), calls=%async_computation.23 | async-start | bytes 2621440 | tf_op jit(solution)/shard_map/reduce_scatter | solution.py:22
  719.5 126.8 %copy-start.2 = (bf16[2,64,2048]{2,1,0:T(8,128)(2,1)S(1)}, bf16[2,64,2048]{2,1,0:T(8,128)(2,1)}, u32[]{:S(2)}) copy-start(bf16[2,64,2048]{2,1,0:T(8,128)(2,1)} %param.16) | copy-start | bytes 1572868
  824.4 11.9 all-to-all-start.1
  836.9 11.7 all-to-all-start
  840.5 41.8 %all-gather.34.cloned.1.call-start = ((), (), s32[]{:S(2)}) async-start(), calls=%async_computation.30 | async-start | bytes 2621440 | tf_op jit(solution)/shard_map/all_gather | solution.py:18
  848.6 121.6 %reduce-scatter.25.cloned.1.call-start = ((), (), s32[]{:S(2)}) async-start(), calls=%async_computation.29 | async-start | bytes 4718592 | tf_op jit(solution)/shard_map/reduce_scatter | solution.py:30
  881.8 121.6 %reduce-scatter.27.cloned.1.call-start = ((), (), s32[]{:S(2)}) async-start(), calls=%async_computation.31 | async-start | bytes 2621440 | tf_op jit(solution)/shard_map/reduce_scatter | solution.py:22
  902.5 193.3 %reduce-scatter.23.cloned.1.call-start = ((), (), s32[]{:S(2)}) async-start(), calls=%async_computation.27 | async-start | bytes 4718592 | tf_op jit(solution)/shard_map/reduce_scatter | solution.py:30
  907.6 188.3 %copy-start.10 = (bf16[128,2048]{1,0:T(8,128)(2,1)S(1)}, bf16[128,2048]{1,0:T(8,128)(2,1)}, u32[]{:S(2)}) copy-start(bf16[128,2048]{1,0:T(8,128)(2,1)} %reduce-scatter.21.cloned.1.call-done) | copy-start | bytes 1572868
  907.6 214.0 %all-gather.36.cloned.1.call-start = ((), (), s32[]{:S(2)}) async-start(), calls=%async_computation.32 | async-start | bytes 2621440 | tf_op jit(solution)/shard_map/all_gather | solution.py:18
  1099.3 78.0 %reduce-scatter.29.cloned.1.call-start = ((), (), s32[]{:S(2)}) async-start(), calls=%async_computation.33 | async-start | bytes 2621440 | tf_op jit(solution)/shard_map/reduce_scatter | solution.py:22
  1145.9 88.7 %reduce-scatter.41.cloned.1.call-start = ((), (), s32[]{:S(2)}) async-start(), calls=%async_computation.39 | async-start | bytes 7208960 | tf_op jit(solution)/shard_map/reduce_scatter | solution.py:188
  1157.1 143.2 %reduce-scatter.45.cloned.1.call-start = ((), (), s32[]{:S(2)}) async-start(), calls=%async_computation.41 | async-start | bytes 73728
  1163.9 250.7 %reduce-scatter.37.cloned.1.call-start = ((), (), s32[]{:S(2)}) async-start(), calls=%async_computation.37 | async-start | bytes 6488064 | tf_op jit(solution)/shard_map/reduce_scatter | solution.py:188
  1171.3 315.0 %reduce-scatter.33.cloned.1.call-start = ((), (), s32[]{:S(2)}) async-start(), calls=%async_computation.35 | async-start | bytes 2359296 | tf_op jit(solution)/shard_map/reduce_scatter | solution.py:188
  1176.6 448.2 %reduce-scatter.43.cloned.1.call-start = ((), (), s32[]{:S(2)}) async-start(), calls=%async_computation.40 | async-start | bytes 1081344
  1180.1 533.8 %reduce-scatter.39.cloned.1.call-start = ((), (), s32[]{:S(2)}) async-start(), calls=%async_computation.38 | async-start | bytes 14417920 | tf_op jit(solution)/shard_map/reduce_scatter | solution.py:188
  1198.5 637.5 %reduce-scatter.31.cloned.1.call-start = ((), (), s32[]{:S(2)}) async-start(), calls=%async_computation.34 | async-start | bytes 7077888 | tf_op jit(solution)/shard_map/reduce_scatter | solution.py:188
  1206.3 825.7 %reduce-scatter.35.cloned.1.call-start = ((), (), s32[]{:S(2)}) async-start(), calls=%async_computation.36 | async-start | bytes 12976128 | tf_op jit(solution)/shard_map/reduce_scatter | solution.py:188
  1219.6 268.5 %copy-start.6 = (f32[128,2048]{1,0:T(8,128)S(1)}, f32[128,2048]{1,0:T(8,128)}, u32[]{:S(2)}) copy-start(f32[128,2048]{1,0:T(8,128)} %get-tuple-element.99) | copy-start | bytes 3145732
  1219.6 268.5 %copy-start.19 = (bf16[128,2048]{1,0:T(8,128)(2,1)S(1)}, bf16[128,2048]{1,0:T(8,128)(2,1)}, u32[]{:S(2)}) copy-start(bf16[128,2048]{1,0:T(8,128)(2,1)} %reduce-scatter.29.cloned.1.call-done) | copy-start | bytes 1572868
  (39 other events, 1049.1 us)
Sparse Core Ops, SparseCore 0:
  54.9 18.6 all-gather.13
  75.8 98.6 all-gather.15
  176.6 48.5 all-gather.17
  229.5 29.3 reduce-scatter.18
  262.5 22.5 all-gather.19
  287.1 163.2 all-gather.21
  452.5 91.3 all-gather.23
  545.4 74.3 all-gather.27
  622.5 72.7 all-gather.25
  697.3 71.3 all-gather.31
  770.2 41.9 all-gather.29
  815.1 31.1 reduce-scatter.20
  848.7 22.5 all-gather.33
  881.9 88.2 reduce-scatter.24
  972.6 30.7 reduce-scatter.26
  1007.4 88.3 reduce-scatter.22
  1099.4 22.1 all-gather.35
  1146.0 31.1 reduce-scatter.28
  1179.8 54.7 reduce-scatter.40
  1237.8 62.4 reduce-scatter.44
  1304.5 110.0 reduce-scatter.36
  1418.1 68.1 reduce-scatter.32
  1489.2 135.5 reduce-scatter.42
  1627.2 86.5 reduce-scatter.38
  1717.5 118.4 reduce-scatter.30
  1839.4 192.4 reduce-scatter.34

commit v2 on v1

--- a/solution.py
+++ b/solution.py
@@ -1,6 +1,11 @@
+import functools
+import itertools
+
 import jax
 import jax.numpy as jnp
 from jax import lax
+from jax.experimental import pallas as pl
+from jax.experimental.pallas import tpu as pltpu
 from jax.sharding import PartitionSpec as P
 
 HD = 128
@@ -8,26 +13,374 @@
 ROPE_BASE = 1000000.0
 F32 = jnp.float32
 BF16 = jnp.bfloat16
+MESH = pl.DeviceIdType.MESH
+VMEM_BYTES = 62 * 1024 * 1024
+
+
+def part(ref, dim, index, size):
+    start = index * size
+    if size % 128 == 0:
+        start = pl.multiple_of(start, 128)
+    elif size % 8 == 0:
+        start = pl.multiple_of(start, 8)
+    return ref.at[tuple(pl.ds(start, size) if i == dim else slice(None) for i in range(len(ref.shape)))]
+
+
+def greet(sizes):
+    barrier = pltpu.get_barrier_semaphore()
+    total = 0
+    for axis, size in sizes.items():
+        me = lax.axis_index(axis)
+        half, side, place = size // 2, me % 2, me // 2
+        for step in range(1, half):
+            peer = (place + step) % half * 2 + side
+            pl.semaphore_signal(barrier, inc=1, device_id={axis: peer}, device_id_type=MESH)
+        pl.semaphore_signal(barrier, inc=1, device_id={axis: me + 1 - 2 * side}, device_id_type=MESH)
+        total += half
+    pl.semaphore_wait(barrier, total)
+
+
+def gather_kernel(plan, sizes, *refs):
+    count = len(plan)
+    ins, outs, stage = refs[:count], refs[count : 2 * count], refs[2 * count : 3 * count]
+    send_sem, recv_sem, near_sem = refs[3 * count :]
+    greet(sizes)
+    base, slot = [0], [0]
+    for axis, dim, first in plan:
+        base.append(base[-1] + sizes[axis])
+        slot.append(slot[-1] + 3 * sizes[axis])
+    loads = []
+    for i in range(count):
+        load = pltpu.make_async_copy(ins[i], stage[i], near_sem.at[i, 0])
+        load.start()
+        loads.append(load)
+    waits = []
+
+    def copy_of(i, src, piece, device, number):
+        axis, dim, first = plan[i]
+        return pltpu.make_async_remote_copy(
+            src_ref=src,
+            dst_ref=part(outs[i], dim, piece, ins[i].shape[dim]),
+            send_sem=send_sem.at[slot[i] + number],
+            recv_sem=recv_sem.at[base[i] + piece],
+            device_id={axis: device},
+            device_id_type=MESH,
+        )
+
+    def push(i, src, piece, device, number, when=None):
+        if when is None:
+            copy_of(i, src, piece, device, number).start()
+        else:
+            pl.when(when)(lambda: copy_of(i, src, piece, device, number).start())
+        waits.append((i, src, piece, device, number, when))
+
+    def arrive(i, piece):
+        axis, dim, first = plan[i]
+        view = part(outs[i], dim, piece, ins[i].shape[dim])
+        copy_of(i, view, piece, lax.axis_index(axis), 0).wait_recv()
+        return view
+
+    def where(i):
+        axis = plan[i][0]
+        me = lax.axis_index(axis)
+        return me, sizes[axis] // 2, me % 2, me // 2
+
+    def chain(i, src, piece, number, left, right):
+        me, half, side, place = where(i)
+        if right is not False:
+            push(i, src, piece, me + 2, number, place < half - 1 if right is True else right)
+        if left is not False:
+            push(i, src, piece, me - 2, number + 1, place > 0 if left is True else left)
+
+    for i, (axis, dim, first) in enumerate(plan):
+        me, half, side, place = where(i)
+        push(i, ins[i], me, me + 1 - 2 * side, 0)
+        if half > 1:
+            chain(i, ins[i], me, 1, True, True)
+    stores = []
+    for i, (axis, dim, first) in enumerate(plan):
+        loads[i].wait()
+        store = pltpu.make_async_copy(
+            stage[i], part(outs[i], dim, lax.axis_index(axis), ins[i].shape[dim]), near_sem.at[i, 1]
+        )
+        store.start()
+        stores.append(store)
+    for i, (axis, dim, first) in enumerate(plan):
+        me, half, side, place = where(i)
+        mate = me + 1 - 2 * side
+        number = 3
+        if first:
+            view = arrive(i, mate)
+            chain(i, view, mate, number, True, True)
+            number += 2
+        for step in range(1, half):
+            for turn in (-1, 1):
+                ok = place >= step if turn < 0 else place < half - step
+                on = (ok & (place < half - 1)) if turn < 0 else (ok & (place > 0))
+                for flip in (False, True) if first else (False,):
+                    piece = (mate if flip else me) + 2 * turn * step
+
+                    @pl.when(ok)
+                    def _(i=i, piece=piece):
+                        arrive(i, piece)
+
+                    view = part(outs[i], dim, piece, ins[i].shape[dim])
+                    if step < half - 1:
+                        push(i, view, piece, me - 2 * turn, number, on)
+                        number += 1
+                    if not first:
+                        push(i, view, piece, mate, number, ok)
+                        number += 1
+    for i, (axis, dim, first) in enumerate(plan):
+        me, half, side, place = where(i)
+        if not first:
+            for step in range(half):
+                arrive(i, (place + step) % half * 2 + 1 - side)
+    for i, src, piece, device, number, when in waits:
+        if when is None:
+            copy_of(i, src, piece, device, number).wait_send()
+        else:
+            pl.when(when)(lambda: copy_of(i, src, piece, device, number).wait_send())
+    for store in stores:
+        store.wait()
+
+
+def aligned(size, array, dim):
+    return size % (128 if dim == array.ndim - 1 else 16) == 0
+
+
+def gather_arrays(arrays, plan, sizes, collective_id):
+    fit = [aligned(a.shape[p[1]], a, p[1]) for a, p in zip(arrays, plan)]
+    if not all(fit):
+        taken = [(a, p) for a, p, ok in zip(arrays, plan, fit) if ok]
+        made = iter(gather_arrays([a for a, _ in taken], tuple(p for _, p in taken), sizes, collective_id))
+        return [
+            next(made) if ok else lax.all_gather(a, p[0], axis=p[1], tiled=True)
+            for a, p, ok in zip(arrays, plan, fit)
+        ]
+
+    def full(array, axis, dim):
+        return tuple(n * sizes[axis] if i == dim else n for i, n in enumerate(array.shape))
+
+    slots = sum(sizes[axis] for axis, _, _ in plan)
+    used = {axis: sizes[axis] for axis in sizes if any(a == axis for a, _, _ in plan)}
+    return pl.pallas_call(
+        functools.partial(gather_kernel, plan, used),
+        out_shape=[jax.ShapeDtypeStruct(full(a, p[0], p[1]), a.dtype) for a, p in zip(arrays, plan)],
+        in_specs=[pl.BlockSpec(memory_space=pl.ANY)] * len(arrays),
+        out_specs=[pl.BlockSpec(memory_space=pl.ANY)] * len(arrays),
+        scratch_shapes=[pltpu.VMEM(a.shape, a.dtype) for a in arrays]
+        + [
+            pltpu.SemaphoreType.DMA((3 * slots,)),
+            pltpu.SemaphoreType.DMA((slots,)),
+            pltpu.SemaphoreType.DMA((len(arrays), 2)),
+        ],
+        compiler_params=pltpu.CompilerParams(
+            collective_id=collective_id, has_side_effects=True, vmem_limit_bytes=VMEM_BYTES
+        ),
+    )(*arrays)
+
+
+def add_into(acc, other, shape):
+    lead = shape[:-2]
+    rows, cols = shape[-2:]
+    block = 32
+    while rows % block:
+        block //= 2
+    outer = 1
+    for n in lead:
+        outer *= n
+    for index in itertools.product(*[range(n) for n in lead]):
+        def step(r, carry, index=index):
+            at = index + (pl.ds(pl.multiple_of(r * block, block), block), slice(None))
+            acc[at] = (acc[at].astype(F32) + other[at].astype(F32)).astype(acc.dtype)
+            return carry
+        lax.fori_loop(0, rows // block, step, 0)
+
+
+def fold_kernel(plan, sizes, order, *refs):
+    count = len(plan)
+    ins, outs = refs[:count], refs[count : 2 * count]
+    across, along, stage = (refs[(2 + j) * count : (3 + j) * count] for j in range(3))
+    x_send, x_recv, z_send, z_recv, load_sem, out_sem = refs[5 * count :]
+    greet(sizes)
+    xbase, zbase, sbase = [0], [0], [0]
+    for axis, dim in plan:
+        half = sizes[axis] // 2
+        xbase.append(xbase[-1] + half)
+        zbase.append(zbase[-1] + half + 1)
+        sbase.append(sbase[-1] + 2 * half)
+
+    def where(i):
+        axis = plan[i][0]
+        me = lax.axis_index(axis)
+        return me, sizes[axis] // 2, me % 2, me // 2
+
+    def size(i):
+        axis, dim = plan[i]
+        return ins[i].shape[dim] // sizes[axis]
+
+    def exchange(i, place):
+        me, half, side, _ = where(i)
+        return pltpu.make_async_remote_copy(
+            src_ref=part(ins[i], plan[i][1], place * 2 + 1 - side, size(i)),
+            dst_ref=across[i].at[place],
+            send_sem=x_send.at[xbase[i] + place],
+            recv_sem=x_recv.at[xbase[i] + place],
+            device_id={plan[i][0]: me + 1 - 2 * side},
+            device_id_type=MESH,
+        )
+
+    def hop(i, owner, turn, dist, number):
+        me, half, side, place = where(i)
+        slot = half if (turn < 0 and dist == 1) else owner
+        return pltpu.make_async_remote_copy(
+            src_ref=across[i].at[owner],
+            dst_ref=along[i].at[slot],
+            send_sem=z_send.at[sbase[i] + number],
+            recv_sem=z_recv.at[zbase[i] + slot],
+            device_id={plan[i][0]: me + 2 * turn},
+            device_id_type=MESH,
+        )
+
+    def landed(i, slot):
+        me, half, side, place = where(i)
+        pltpu.make_async_remote_copy(
+            src_ref=along[i].at[slot], dst_ref=along[i].at[slot], send_sem=z_send.at[0],
+            recv_sem=z_recv.at[zbase[i] + slot], device_id={plan[i][0]: me}, device_id_type=MESH,
+        ).wait_recv()
+
+    tasks = []
+    for i, own in order:
+        axis, dim = plan[i]
+        half = sizes[axis] // 2
+        if own:
+            tasks.append((i, 0, 0))
+        else:
+            tasks += [(i, d, turn) for d in range(half - 1, 0, -1) for turn in (1, -1)]
+
+    def valid(task):
+        i, d, turn = task
+        me, half, side, place = where(i)
+        return None if d == 0 else (place + d < half if turn > 0 else place >= d)
+
+    def guard(cond, fn):
+        if cond is None:
+            fn()
+        else:
+            pl.when(cond)(fn)
+
+    parity = {}
+    slots = []
+    for task in tasks:
+        parity[task[0]] = parity.get(task[0], -1) + 1
+        slots.append(parity[task[0]] % 2)
+
+    def load(n):
+        i, d, turn = tasks[n]
+        me, half, side, place = where(i)
+        owner = place + turn * d
+        return pltpu.make_async_copy(
+            part(ins[i], plan[i][1], owner * 2 + side, size(i)), stage[i].at[slots[n]], load_sem.at[i, slots[n]]
+        )
+
+    guard(valid(tasks[0]), lambda: load(0).start())
+    pushed = set()
+    for i, own in order:
+        if i in pushed:
+            continue
+        pushed.add(i)
+        me, half, side, place = where(i)
+        for d in range(half - 1, 0, -1):
+            for turn in (1, -1):
+                owner = place + turn * d
+                pl.when(owner < half if turn > 0 else owner >= 0)(lambda i=i, owner=owner: exchange(i, owner).start())
+        exchange(i, place).start()
+    for n, task in enumerate(tasks):
+        i, d, turn = task
+        me, half, side, place = where(i)
+        owner = place + turn * d
+        shape = stage[i].shape[1:]
+        if n + 1 < len(tasks):
+            guard(valid(tasks[n + 1]), lambda n=n: load(n + 1).start())
+
+        def work(n=n, i=i, d=d, turn=turn, owner=owner, shape=shape, half=half, place=place):
+            exchange(i, owner).wait_recv()
+            load(n).wait()
+            add_into(across[i].at[owner], stage[i].at[slots[n]], shape)
+            if d == 0:
+                if half > 1:
+                    for cond, slot in ((place > 0, place), (place < half - 1, half)):
+                        @pl.when(cond)
+                        def _(slot=slot):
+                            landed(i, slot)
+                            add_into(across[i].at[owner], along[i].at[slot], shape)
+                pltpu.make_async_copy(across[i].at[owner], outs[i], out_sem.at[i]).start()
+            else:
+                @pl.when(place > 0 if turn > 0 else place < half - 1)
+                def _():
+                    landed(i, owner)
+                    add_into(across[i].at[owner], along[i].at[owner], shape)
+                hop(i, owner, turn, d, 2 * (d - 1) + (turn > 0)).start()
+
+        guard(valid(task), work)
+    for i, d, turn in tasks:
+        me, half, side, place = where(i)
+        owner = place + turn * d
+        if d:
+            guard(valid((i, d, turn)), lambda i=i, owner=owner, turn=turn, d=d: hop(i, owner, turn, d, 2 * (d - 1) + (turn > 0)).wait_send())
+    for i in range(count):
+        me, half, side, place = where(i)
+        for p in range(half):
+            exchange(i, p).wait_send()
+        pltpu.make_async_copy(across[i].at[place], outs[i], out_sem.at[i]).wait()
+
+
+def fold_arrays(arrays, plan, sizes, order, collective_id):
+    fit = [aligned(a.shape[p[1]] // sizes[p[0]], a, p[1]) for a, p in zip(arrays, plan)]
+    if not all(fit):
+        taken = [i for i, ok in enumerate(fit) if ok]
+        kept = tuple((taken.index(i), own) for i, own in order if fit[i])
+        made = iter(
+            fold_arrays([arrays[i] for i in taken], tuple(plan[i] for i in taken), sizes, kept, collective_id)
+        )
+        return [
+            next(made) if ok else lax.psum_scatter(a, p[0], scatter_dimension=p[1], tiled=True)
+            for a, p, ok in zip(arrays, plan, fit)
+        ]
+
+    used = {axis: sizes[axis] for axis in sizes if any(a == axis for a, _ in plan)}
+    half = [sizes[axis] // 2 for axis, _ in plan]
+    piece = [
+        tuple(n // sizes[axis] if j == dim else n for j, n in enumerate(a.shape))
+        for a, (axis, dim) in zip(arrays, plan)
+    ]
+    kinds = [a.dtype for a in arrays]
+    dma = pltpu.SemaphoreType.DMA
+    return pl.pallas_call(
+        functools.partial(fold_kernel, plan, used, order),
+        out_shape=[jax.ShapeDtypeStruct(p, k) for p, k in zip(piece, kinds)],
+        in_specs=[pl.BlockSpec(memory_space=pl.ANY)] * len(arrays),
+        out_specs=[pl.BlockSpec(memory_space=pl.ANY)] * len(arrays),
+        scratch_shapes=[pltpu.VMEM((h,) + p, k) for h, p, k in zip(half, piece, kinds)]
+        + [pltpu.VMEM((h + 1,) + p, k) for h, p, k in zip(half, piece, kinds)]
+        + [pltpu.VMEM((2,) + p, k) for p, k in zip(piece, kinds)]
+        + [
+            dma((sum(half),)),
+            dma((sum(half),)),
+            dma((2 * sum(half),)),
+            dma((sum(half) + len(half),)),
+            dma((len(half), 2)),
+            dma((len(half),)),
+        ],
+        compiler_params=pltpu.CompilerParams(
+            collective_id=collective_id, has_side_effects=True, vmem_limit_bytes=67043328
+        ),
+    )(*arrays)
 
 
 def dot(spec, left, right):
     return jnp.einsum(spec, left, right, preferred_element_type=F32)
-
-
-def spread_rows(rows):
-    return lax.all_gather(rows, "shard", axis=0, tiled=True)
-
-
-def fold_rows(rows):
-    return lax.psum_scatter(rows.astype(BF16), "shard", scatter_dimension=0, tiled=True).astype(F32)
-
-
-def spread_experts(rows):
-    return lax.all_gather(rows, "expert", axis=0, tiled=True)
-
-
-def fold_experts(rows):
-    return lax.psum_scatter(rows.astype(BF16), "expert", scatter_dimension=0, tiled=True).astype(F32)
 
 
 def rotate(tensor, cosine, sine):
@@ -66,27 +419,39 @@
     vectors = jnp.stack([gain_attn, gain_ffn, shared_gate])
     vectors = lax.all_gather(vectors, ("expert", "shard"), axis=1, tiled=True)
     bias = lax.all_gather(b_qkv, "expert", axis=2, tiled=True)
-    qkv = lax.all_gather(w_qkv, "expert", axis=1, tiled=True)
-    out = lax.all_gather(w_out, "expert", axis=1, tiled=True)
-    sgu = lax.all_gather(w_sgu, "expert", axis=1, tiled=True)
-    sd = lax.all_gather(w_sd, "expert", axis=1, tiled=True)
-    egu = lax.all_gather(w_egu, "shard", axis=2, tiled=True)
-    ed = lax.all_gather(w_ed, "shard", axis=1, tiled=True)
+    sizes = {"expert": lax.axis_size("expert"), "shard": shards}
+    low_rows = tokens.reshape(count, width)
+    grad_low = cotangent.reshape(count, width)
+    source_rows, grad_low_rows, egu, ed, qkv, sgu, sd, out = gather_arrays(
+        (low_rows, grad_low, w_egu, w_ed, w_qkv, w_sgu, w_sd, w_out),
+        (
+            ("shard", 0, False),
+            ("shard", 0, False),
+            ("shard", 2, False),
+            ("shard", 1, False),
+            ("expert", 1, False),
+            ("expert", 1, False),
+            ("expert", 1, True),
+            ("expert", 1, False),
+        ),
+        sizes,
+        0,
+    )
 
     gain_one, gain_two, gate_vec = (vectors[i].astype(F32) for i in range(3))
-    source = tokens.reshape(count, width).astype(F32)
-    grad_low = cotangent.reshape(count, width)
+    source = low_rows.astype(F32)
     grad_out = grad_low.astype(F32)
     chosen = (routes.reshape(count, -1)[:, :, None] == jnp.arange(experts)).astype(F32)
     gates = jnp.sum(chosen * gate_weight.reshape(count, -1)[:, :, None], axis=1)
     gates = gates.T.reshape(-1, own, count)
     gates = lax.all_to_all(gates, "expert", split_axis=0, concat_axis=0, tiled=True)
     gates = gates.transpose(1, 0, 2).reshape(own, -1)
-    grad_all = spread_experts(grad_low)
+    grad_all = lax.all_gather(grad_low, "expert", axis=0, tiled=True)
 
     scale_one = lax.rsqrt(jnp.mean(source * source, axis=-1, keepdims=True) + EPSILON)
-    normed_one = (source * scale_one * gain_one).astype(BF16)
-    rows_one = spread_rows(normed_one)
+    rows_one = source_rows.astype(F32)
+    rows_scale = lax.rsqrt(jnp.mean(rows_one * rows_one, axis=-1, keepdims=True) + EPSILON)
+    rows_one = (rows_one * rows_scale * gain_one).astype(BF16)
     projected = dot("ld,ide->ile", rows_one, qkv) + bias.reshape(3, 1, -1).astype(F32)
 
     place = jnp.arange(length).astype(F32)
@@ -116,23 +481,36 @@
     exact = expo / total
     probs = exact.astype(BF16)
     context = to_rows(dot("mhqk,mhkd->mhqd", probs, values).astype(BF16))
-    hidden = source + fold_rows(dot("le,ed->ld", context, out))
+    attended = dot("le,ed->ld", context, out).astype(BF16)
+    (attended,) = fold_arrays((attended,), (("shard", 0),), sizes, ((0, False), (0, True)), 1)
+    hidden = source + attended.astype(F32)
 
     scale_two = lax.rsqrt(jnp.mean(hidden * hidden, axis=-1, keepdims=True) + EPSILON)
     normed_two = (hidden * scale_two * gain_two).astype(BF16)
-    rows_two = spread_rows(normed_two)
-    routed = spread_experts(normed_two)
+    (rows_two,) = gather_arrays((normed_two,), (("shard", 0, False),), sizes, 2)
+    routed = lax.all_gather(normed_two, "expert", axis=0, tiled=True)
     shared_in = dot("ld,idf->ilf", rows_two, sgu)
     shared_act = (jax.nn.silu(shared_in[0]) * shared_in[1]).astype(BF16)
-    shared_sum = fold_rows(dot("lf,fd->ld", shared_act, sd))
+    shared_part = dot("lf,fd->ld", shared_act, sd).astype(BF16)
     normed_float = normed_two.astype(F32)
     opening = jax.nn.sigmoid(jnp.sum(normed_float * gate_vec, axis=-1))
+    opening_rows = jax.nn.sigmoid(jnp.sum(rows_two.astype(F32) * gate_vec, axis=-1))
+
+    grad_shared_rows = (opening_rows[:, None] * grad_low_rows.astype(F32)).astype(BF16)
+    grad_shared_act = dot("ld,fd->lf", grad_shared_rows, sd)
+    grad_sd = dot("lf,ld->fd", shared_act, grad_shared_rows).astype(BF16)
+    grad_shared_in = swish_back(shared_in[0], shared_in[1], grad_shared_act)
+    grad_sgu = dot("ld,ilf->idf", rows_two, grad_shared_in).astype(BF16)
+    grad_from_shared = dot("ilf,idf->ld", grad_shared_in, sgu).astype(BF16)
+    routed, grad_sd, grad_sgu, grad_from_shared, shared_part = lax.optimization_barrier(
+        (routed, grad_sd, grad_sgu, grad_from_shared, shared_part)
+    )
 
     expert_in = dot("rd,jidf->ijrf", routed, egu)
     expert_act = (jax.nn.silu(expert_in[0]) * expert_in[1]).astype(BF16)
     expert_out = dot("jrf,jfd->jrd", expert_act, ed).astype(BF16).astype(F32)
-    blend = fold_experts(jnp.sum(gates[:, :, None] * expert_out, axis=0))
-    mixed = hidden + opening[:, None] * shared_sum + blend
+    blend = jnp.sum(gates[:, :, None] * expert_out, axis=0).astype(BF16)
+    blend = lax.psum_scatter(blend, "expert", scatter_dimension=0, tiled=True).astype(F32)
     grad_all_float = grad_all.astype(F32)
     inner = jnp.sum(expert_out * grad_all_float, axis=-1)
     inner = inner.reshape(own, -1, count).transpose(1, 0, 2)
@@ -142,29 +520,31 @@
 
     grad_expert = (gates[:, :, None] * grad_all_float).astype(BF16)
     grad_expert_act = dot("jrd,jfd->jrf", grad_expert, ed)
-    grad_ed = dot("jrf,jrd->jfd", expert_act, grad_expert)
+    grad_ed = dot("jrf,jrd->jfd", expert_act, grad_expert).astype(BF16)
     grad_expert_in = swish_back(expert_in[0], expert_in[1], grad_expert_act)
-    grad_routed = dot("ijrf,jidf->rd", grad_expert_in, egu)
-    grad_egu = dot("rd,ijrf->jidf", routed, grad_expert_in)
-    grad_from_experts = fold_experts(grad_routed)
-
-    grad_shared = (opening[:, None] * grad_out).astype(BF16)
-    grad_shared_rows = spread_rows(grad_shared)
-    grad_shared_act = dot("ld,fd->lf", grad_shared_rows, sd)
-    grad_sd = dot("lf,ld->fd", shared_act, grad_shared_rows)
-    grad_shared_in = swish_back(shared_in[0], shared_in[1], grad_shared_act)
-    grad_sgu = dot("ld,ilf->idf", rows_two, grad_shared_in)
-    grad_from_shared = fold_rows(dot("ilf,idf->ld", grad_shared_in, sgu))
+    grad_routed = dot("ijrf,jidf->rd", grad_expert_in, egu).astype(BF16)
+    grad_egu = dot("rd,ijrf->jidf", routed, grad_expert_in).astype(BF16)
+    grad_routed, grad_egu, grad_ed = lax.optimization_barrier((grad_routed, grad_egu, grad_ed))
+    grad_from_experts, shared_sum, grad_from_shared = fold_arrays(
+        (grad_routed, shared_part, grad_from_shared),
+        (("expert", 0), ("shard", 0), ("shard", 0)),
+        sizes,
+        ((1, False), (2, False), (0, False), (1, True), (2, True), (0, True)),
+        3,
+    )
+    shared_sum = shared_sum.astype(F32)
+    mixed = hidden + opening[:, None] * shared_sum + blend
+
     grad_opening = jnp.sum(grad_out * shared_sum, axis=-1)
     grad_logit = grad_opening * opening * (1.0 - opening)
     grad_gate_vec = jnp.sum(grad_logit[:, None] * normed_float, axis=0)
-    grad_normed_two = grad_from_experts + grad_from_shared + grad_logit[:, None] * gate_vec
+    grad_normed_two = grad_from_experts.astype(F32) + grad_from_shared.astype(F32) + grad_logit[:, None] * gate_vec
     grad_hidden, grad_gain_two = norm_back(grad_normed_two, hidden, scale_two, gain_two)
     grad_hidden = grad_out + grad_hidden
 
-    grad_rows = spread_rows(grad_hidden.astype(BF16))
+    (grad_rows,) = gather_arrays((grad_hidden.astype(BF16),), (("shard", 0, False),), sizes, 4)
     grad_context = to_heads(dot("ld,ed->le", grad_rows, out).astype(BF16))
-    grad_out_w = dot("le,ld->ed", context, grad_rows)
+    grad_out_w = dot("le,ld->ed", context, grad_rows).astype(BF16)
     grad_probs = dot("mhqd,mhkd->mhqk", grad_context, values)
     delta = jnp.sum(exact * grad_probs, axis=-1, keepdims=True)
     grad_scores = (exact * (grad_probs - delta)).astype(BF16)
@@ -179,20 +559,25 @@
         ]
     ).astype(BF16)
     grad_bias = jnp.sum(grad_projected.astype(F32), axis=1).reshape(3, heads, HD)
-    grad_qkv = dot("ld,ile->ide", rows_one, grad_projected)
-    grad_normed_one = fold_rows(dot("ile,ide->ld", grad_projected, qkv))
+    grad_qkv = dot("ld,ile->ide", rows_one, grad_projected).astype(BF16)
+    grad_normed_one = dot("ile,ide->ld", grad_projected, qkv).astype(BF16)
+    (grad_normed_one,) = fold_arrays((grad_normed_one,), (("shard", 0),), sizes, ((0, False), (0, True)), 5)
+    grad_normed_one, grad_qkv, grad_out_w = lax.optimization_barrier((grad_normed_one, grad_qkv, grad_out_w))
+    grad_normed_one = grad_normed_one.astype(F32)
     grad_source, grad_gain_one = norm_back(grad_normed_one, source, scale_one, gain_one)
     grad_tokens = grad_hidden + grad_source
 
-    def fold_weights(value, axis, dim):
-        return lax.psum_scatter(value.astype(BF16), axis, scatter_dimension=dim, tiled=True).astype(F32)
-
-    summed_ed = fold_weights(grad_ed, "shard", 1)
-    summed_egu = fold_weights(grad_egu, "shard", 2)
-    summed_sd = fold_weights(grad_sd, "expert", 1)
-    summed_sgu = fold_weights(grad_sgu, "expert", 1)
-    summed_out = fold_weights(grad_out_w, "expert", 1)
-    summed_qkv = fold_weights(grad_qkv, "expert", 1)
+    folded = fold_arrays(
+        (grad_egu, grad_ed, grad_sgu, grad_qkv, grad_sd, grad_out_w),
+        (("shard", 2), ("shard", 1), ("expert", 1), ("expert", 1), ("expert", 1), ("expert", 1)),
+        sizes,
+        tuple((i, own) for i, own in (
+            (0, False), (1, False), (2, False), (2, True), (3, False), (3, True),
+            (0, True), (1, True), (4, False), (4, True), (5, False), (5, True),
+        )),
+        6,
+    )
+    summed_egu, summed_ed, summed_sgu, summed_qkv, summed_sd, summed_out = (x.astype(F32) for x in folded)
     summed_bias = lax.psum_scatter(grad_bias, "expert", scatter_dimension=2, tiled=True)
     gains = jnp.stack([grad_gain_one, grad_gain_two, grad_gate_vec])
     gains = lax.psum_scatter(gains, ("expert", "shard"), scatter_dimension=1, tiled=True)

time: 2050 us -> 1150 us (0.56)
  waiting for transfers between devices: 1670 us -> 69.6 us
  Pallas kernels: 0 us -> 737 us
  local copies, waits for them, and re-layouts: 49.6 us -> 25.5 us
    reduce_scatter x12 -> x1, waiting for transfers between devices: 816 us -> 0.01 us  [body(): lax.psum_scatter(blend, 'expert', scatter_dimension=0, tiled=True)]
    pallas_call x0 -> x7, Pallas kernels: none -> 737 us  [the longest x4 386 us: fold_arrays(): pl.pallas_call(functools.partial(fold_kernel, plan, used, order), out_sha...]
    all_gather x12 -> x2, waiting for transfers between devices: 641 us -> 57.8 us  [the longest x1 49.9 us: body(): grad_all = lax.all_gather(grad_low, 'expert', axis=0, tiled=True)]
    unnamed x28 -> x7, waiting for transfers between devices: 203 us -> 0.76 us
    unnamed x106 -> x143, local copies, waits for them, and re-layouts: 37.1 us -> 14.2 us
  transfers between devices with their start and end apart: 28 -> 7, of which waited for: 25 -> 4; matrix products, arithmetic and copies ran while one was open for 11% -> 13% of each run, Pallas kernels for 0% -> 32%
where the time goes in v2:
time: 1150 us; the launch traced here: 1140 us
  Pallas kernels  737 us (64%)
  matrix products  167 us (15%)
  waiting for transfers between devices  69.6 us (6%)
  blocking collectives  69.3 us (6%)
  other arithmetic  47.7 us (4%)
  local copies, waits for them, and re-layouts  25.5 us (2%)
  between operations  15.3 us (1%)
    pallas_call x4, Pallas kernels, fold_arrays(): pl.pallas_call(functools.partial(fold_kernel, plan, used, order), out_sha...  386 us
    pallas_call x3, Pallas kernels, gather_arrays(): pl.pallas_call(functools.partial(gather_kernel, plan, used), out_shape=[j...  351 us
    dot_general x23, matrix products, dot(): return jnp.einsum(spec, left, right, preferred_element_type=F32)  164 us
    all_gather x1, waiting for transfers between devices, body(): grad_all = lax.all_gather(grad_low, 'expert', axis=0, tiled=True)  49.9 us
    all_gather x1, blocking collectives, body(): vectors = lax.all_gather(vectors, ('expert', 'shard'), axis=1, tiled=True)  38.8 us
    all_gather x1, blocking collectives, body(): bias = lax.all_gather(b_qkv, 'expert', axis=2, tiled=True)  30.5 us
  transfers between devices with their start and end apart: 7, of which 4 were waited for; matrix products, arithmetic and copies ran while one was open for 13% of the time, Pallas kernels for 32%

profile of v2, /device:TPU:0, one launch (start us, length us, event | category | flops | bytes accessed | tf_op | source)
XLA Modules:
  0.0 1137.4 jit_solution(10369109443518925208)
XLA Ops:
  7.3 317.7 %shard_map.246 = (bf16[512,2048]{1,0:T(8,128)(2,1)}, bf16[512,2048]{1,0:T(8,128)(2,1)}, bf16[1,2,2048,1408]{3,2,1,0:T(8,128)(2,1)}, bf16[1,1408,2048]{2,1,0:T(8,...) custom-call(bf16[128,2048]{1,0:T(8,128)(2,1)} %bitcast.242, ...), custom_call_target="tpu_custom_call" | custom-call | tf_op jit(solution)/shard_map/pallas_call | solution.py:167
  327.2 38.8 %all-gather = bf16[32,64,3]{1,2,0:T(4,128)(2,1)S(1)} all-gather(bf16[1,64,3]{1,2,0:T(4,128)(2,1)S(1)} %maximum_bitcast_fusion), channel_id=1, replica_groups=mesh['expert'=8,'shard'=4] {'expert','shard'}, dimensions={0}, use_global_device_ids=true | all-gather | bytes 12672 | tf_op jit(solution)/shard_map/all_gather | solution.py:420
  366.8 30.5 %all_gather.13 = bf16[3,4,128]{1,0,2:T(4,128)(2,1)S(1)} all-gather(bf16[3,4,16]{1,0,2:T(4,128)(2,1)S(1)} %copy.210), channel_id=1, replica_groups=mesh['expert'=8,'shard'=4] {'expert'}, dimensions={2}, use_global_device_ids=true | all-gather | bytes 3456 | tf_op jit(solution)/shard_map/all_gather | solution.py:421
  397.4 6.4 add_bitcast_fusion
  420.8 16.8 %shard_map.247 = bf16[128,2048]{1,0:T(8,128)(2,1)} custom-call(bf16[512,2048]{1,0:T(8,128)(2,1)} %convolution_convert_fusion.3.refs_0_), custom_call_target="tpu_custom_call" | custom-call | tf_op jit(solution)/shard_map/pallas_call | solution.py:360
  443.2 16.5 %shard_map.248 = bf16[512,2048]{1,0:T(8,128)(2,1)} custom-call(bf16[128,2048]{1,0:T(8,128)(2,1)} %get-tuple-element.146.refs_0_), custom_call_target="tpu_custom_call" | custom-call | tf_op jit(solution)/shard_map/pallas_call | solution.py:167
  461.9 10.0 convolution_bitcast_fusion
  472.0 4.8 fusion.46
  476.8 5.2 convolution_convert_fusion.1.refs_4_
  482.0 4.6 convolution_convert_fusion.4.refs_1_
  486.7 9.9 convert_bitcast_fusion.1.refs_2_
  496.5 7.5 bitcast_convert_fusion.2.refs_2_
  504.1 7.9 all-gather.6.cloned.1.call-done
  511.9 17.2 %fusion.9 = f32[2,1,1024,1408]{3,2,1,0:T(8,128)S(1)} fusion(bf16[1,2,2048,1408]{3,2,1,0:T(8,128)(2,1)} %get-tuple-element.45, bf16[1024,2048]{1,0:T(8,128)(2,1)} %all-gather.6.cloned.1.call-done), kind=kOutput, calls=%fused_computation.17 | convolution fusion | flops 11811160064 | bytes 27262976 | tf_op jit(solution)/shard_map/rd,jidf->ijrf/dot_general | solution.py:383
  529.1 4.2 copy-done.4
  535.5 49.9 %all-gather.4.cloned.1.call-done = bf16[1024,2048]{1,0:T(8,128)(2,1)} async-done(((bf16[128,2048]{1,0:T(8,128)(2,1)}), bf16[1024,2048]{1,0:T(8,128)(2,1)}) %all-gather.4.cloned.1.call-update) | async-done | bytes 4194320 | tf_op jit(solution)/shard_map/all_gather | solution.py:449
  585.4 12.2 %fusion.7 = (f32[1024]{0:T(1024)}, bf16[1024,2048]{1,0:T(8,128)(2,1)}) fusion(bf16[1024,2048]{1,0:T(8,128)(2,1)} %all-gather.4.cloned.1.call-done, bf16[1,1408,2048]{2,1,0:T(8,128)(2,1)} %get-tuple-element.44, bf16[1,1,1024,1408]{3,2,1,0:T(8,128)(2,1)S(1)} %multiply_convert_fusion), kind=kOutput, calls=%fused_computation.12 | convolution fusion | flops 5916064768 | bytes 17043456 | tf_op jit(solution)/shard_map/jrf,jfd->jrd/dot_general | solution.py:383
  601.3 6.0 all-to-all-done.1
  612.5 5.0 all-to-all-done
  617.5 4.9 fusion.6
  622.5 16.3 %fusion.38 = (bf16[1,1024,1408]{2,1,0:T(8,128)(2,1)}, bf16[1,1024,1408]{2,1,0:T(8,128)(2,1)}) fusion(f32[2,1,1024,1408]{3,2,1,0:T(8,128)} %copy-done.4, bf16[1,1408,2048]{2,1,0:T(8,128)(2,1)} %get-tuple-element.44, bf16[1024,2048]{1,0:T(8,128)(2,1)} %all-gather.4.cloned.1.call-done, f32[1024]{0:T(1024)S(1)} %bitcast.284), kind=kOutput, calls=%fused_computation.66 | convolution fusion | flops 5930614784 | bytes 27267072 | tf_op jit(solution)/shard_map/jrd,jfd->jrf/dot_general | solution.py:383
  638.9 8.3 fusion.8.refs_1_
  647.1 18.8 %convert_bitcast_fusion.refs_0_ = bf16[1,2,2048,1408]{3,2,1,0:T(8,128)(2,1)} fusion(bf16[1024,2048]{1,0:T(8,128)(2,1)} %all-gather.6.cloned.1.call-done, bf16[1,1024,1408]{2,1,0:T(8,128)(2,1)} %get-tuple-element.148, bf16[1,1024,1408]{2,1,0:T(8,128)(2,1)} %get-tuple-element.147), kind=kOutput, calls=%fused_computation.5 | convolution fusion | flops 11819810816 | bytes 21495808 | tf_op jit(solution)/shard_map/rd,ijrf->jidf/dot_general | solution.py:383
  666.0 15.2 %bitcast_convert_fusion.refs_0_ = bf16[1024,2048]{1,0:T(8,128)(2,1)} fusion(bf16[1,2,2048,1408]{3,2,1,0:T(8,128)(2,1)S(1)} %bitcast.295, bf16[1,1024,1408]{2,1,0:T(8,128)(2,1)} %get-tuple-element.148, bf16[1,1024,1408]{2,1,0:T(8,128)(2,1)} %get-tuple-element.147), kind=kOutput, calls=%fused_computation.13 | convolution fusion | flops 11816140800 | bytes 21495808 | tf_op jit(solution)/shard_map/ijrf,jidf->rd/dot_general | solution.py:383
  681.2 63.8 %shard_map.249 = (bf16[128,2048]{1,0:T(8,128)(2,1)}, bf16[128,2048]{1,0:T(8,128)(2,1)}, bf16[128,2048]{1,0:T(8,128)(2,1)}) custom-call(bf16[1024,2048]{1,0:T(8,128)(2,1)} %bitcast_convert_fusion.refs_0_, bf16[512,2048]{1,0:T(8,128)(2,1)} %convolution_convert_fusion.4.refs_1_, bf16[512,2048]{1,0:T(8,128)(2,1)} %bitcast_convert_fusion.2.refs_2_), custom_call_target="tpu_custom_call" | custom-call | tf_op jit(solution)/shard_map/pallas_call | solution.py:360
  753.7 16.4 %shard_map.250 = bf16[512,2048]{1,0:T(8,128)(2,1)} custom-call(bf16[128,2048]{1,0:T(8,128)(2,1)} %get-tuple-element.141.refs_0_), custom_call_target="tpu_custom_call" | custom-call | tf_op jit(solution)/shard_map/pallas_call | solution.py:167
  770.2 4.5 convolution_convert_fusion.2.refs_5_
  786.0 7.6 convert_bitcast_fusion.2.refs_3_
  793.6 7.4 bitcast_convert_fusion.1.refs_0_
  801.8 17.5 %shard_map.251 = bf16[128,2048]{1,0:T(8,128)(2,1)} custom-call(bf16[512,2048]{1,0:T(8,128)(2,1)} %bitcast_convert_fusion.1.refs_0_), custom_call_target="tpu_custom_call" | custom-call | tf_op jit(solution)/shard_map/pallas_call | solution.py:360
  826.4 287.8 %shard_map.252 = (bf16[1,2,512,1408]{3,2,1,0:T(8,128)(2,1)}, bf16[1,352,2048]{2,1,0:T(8,128)(2,1)}, bf16[2,256,1408]{2,1,0:T(8,128)(2,1)}, bf16[3,256,512]{2,1,0...) custom-call(bf16[1,2,2048,1408]{3,2,1,0:T(8,128)(2,1)} %convert_bitcast_fusion.refs_0_, ...), custom_call_target="tpu_custom_call" | custom-call | tf_op jit(solution)/shard_map/pallas_call | solution.py:360
  1114.2 4.8 convert_element_type.332
  (235 shorter events, 77.6 us)
Async XLA Ops:
  7.2 504.7 %all-gather.6.cloned.1.call-start = ((), (), s32[]{:S(2)}) async-start(), calls=%async_computation.6 | async-start | bytes 4718592 | tf_op jit(solution)/shard_map/all_gather | solution.py:491
  7.3 319.9 %copy-start.48 = (bf16[64]{0:T(256)(128)(2,1)S(1)}, bf16[64]{0:T(256)(128)(2,1)}, u32[]{:S(2)}) copy-start(bf16[64]{0:T(256)(128)(2,1)} %param.27) | copy-start | bytes 388
  7.3 319.9 %copy-start.49 = (bf16[64]{0:T(256)(128)(2,1)S(1)}, bf16[64]{0:T(256)(128)(2,1)}, u32[]{:S(2)}) copy-start(bf16[64]{0:T(256)(128)(2,1)} %param.24) | copy-start | bytes 388
  7.3 319.9 %copy-start.50 = (bf16[64]{0:T(256)(128)(2,1)S(1)}, bf16[64]{0:T(256)(128)(2,1)}, u32[]{:S(2)}) copy-start(bf16[64]{0:T(256)(128)(2,1)} %param.20) | copy-start | bytes 388
  7.3 359.4 %copy-start.43 = (bf16[3,4,16]{2,1,0:T(4,128)(2,1)S(1)}, bf16[3,4,16]{2,1,0:T(4,128)(2,1)}, u32[]{:S(2)}) copy-start(bf16[3,4,16]{2,1,0:T(4,128)(2,1)} %param.22) | copy-start | bytes 1156
  327.1 76.7 %copy-start.46 = (f32[512]{0:T(512)}, f32[512]{0:T(512)S(1)}, u32[]{:S(2)}) copy-start(f32[512]{0:T(512)S(1)} %add_rsqrt_fusion) | copy-start | bytes 6148
  366.7 37.2 %copy-start.34 = (f32[1,2048]{1,0:T(1,128)}, f32[1,2048]{1,0:T(1,128)S(1)}, u32[]{:S(2)}) copy-start(f32[1,2048]{1,0:T(1,128)S(1)} %get-tuple-element.170) | copy-start | bytes 24580
  439.0 20.6 %copy-start.31 = (f32[1,2048]{1,0:T(1,128)S(1)}, f32[1,2048]{1,0:T(1,128)}, u32[]{:S(2)}) copy-start(f32[1,2048]{1,0:T(1,128)} %get-tuple-element.171) | copy-start | bytes 24580
  442.4 143.0 %all-gather.4.cloned.1.call-start = ((), (), s32[]{:S(2)}) async-start(), calls=%async_computation.5 | async-start | bytes 4718592 | tf_op jit(solution)/shard_map/all_gather | solution.py:449
  459.7 12.3 %slice-start.6 = ((s8[5767168]{0:T(1024)(128)(4,1)}), s8[4194304]{0:T(1024)(128)(4,1)S(1)}, s32[]{:S(2)}) async-start(s8[5767168]{0:T(1024)(128)(4,1)} %bitcast.298), calls=%async_computation.16 | async-start | bytes 8388608
  461.9 10.0 slice-start.7
  461.9 10.0 copy-start.54
  482.0 14.5 %slice-start.3 = ((s8[11534336]{0:T(1024)(128)(4,1)}), s8[4194304]{0:T(1024)(128)(4,1)S(1)}, s32[]{:S(2)}) async-start(s8[11534336]{0:T(1024)(128)(4,1)} %bitcast.296), calls=%async_computation.13 | async-start | bytes 8388608
  486.7 9.9 slice-start.4
  486.7 9.9 slice-start.5
  585.4 15.5 %copy-start = (bf16[2,64,2048]{2,1,0:T(8,128)(2,1)S(1)}, bf16[2,64,2048]{2,1,0:T(8,128)(2,1)}, u32[]{:S(2)}) copy-start(bf16[2,64,2048]{2,1,0:T(8,128)(2,1)} %param.15) | copy-start | bytes 1572868
  585.4 15.7 %copy-start.41 = (s32[2,64,4]{1,2,0:T(4,128)S(1)}, s32[2,64,4]{1,2,0:T(4,128)}, u32[]{:S(2)}) copy-start(s32[2,64,4]{1,2,0:T(4,128)} %param.18) | copy-start | bytes 6148
  585.4 15.8 %copy-start.42 = (f32[2,64,4]{1,2,0:T(4,128)S(1)}, f32[2,64,4]{1,2,0:T(4,128)}, u32[]{:S(2)}) copy-start(f32[2,64,4]{1,2,0:T(4,128)} %param.19) | copy-start | bytes 6148
  597.6 9.7 all-to-all-start.1
  607.9 9.7 all-to-all-start
  611.2 139.2 %reduce-scatter.8.cloned.1.call-start = ((), (), s32[]{:S(2)}) async-start(), calls=%async_computation.7 | async-start | bytes 4718592 | tf_op jit(solution)/shard_map/reduce_scatter | solution.py:513
  622.5 503.8 %reduce-scatter.12.cloned.1.call-start = ((), (), s32[]{:S(2)}) async-start(), calls=%async_computation.9 | async-start | bytes 73728
  622.5 16.3 %copy-start.51 = (bf16[1024,2048]{1,0:T(8,128)(2,1)S(1)}, bf16[1024,2048]{1,0:T(8,128)(2,1)}, u32[]{:S(2)}) copy-start(bf16[1024,2048]{1,0:T(8,128)(2,1)} %all-gather.4.cloned.1.call-done) | copy-start | bytes 12582916
  638.8 27.1 %slice-start = ((s8[11534336]{0:T(1024)(128)(4,1)}), s8[4194304]{0:T(1024)(128)(4,1)S(1)}, s32[]{:S(2)}) async-start(s8[11534336]{0:T(1024)(128)(4,1)} %bitcast.294), calls=%async_computation.10 | async-start | bytes 8388608
  647.1 18.8 %slice-start.1 = ((s8[11534336]{0:T(1024)(128)(4,1)}), s8[4194304]{0:T(1024)(128)(4,1)S(1)}, s32[]{:S(2)}) async-start(s8[11534336]{0:T(1024)(128)(4,1)} %bitcast.294), calls=%async_computation.11 | async-start | bytes 8388608
  647.1 18.8 %slice-start.2 = ((s8[11534336]{0:T(1024)(128)(4,1)}), s8[3145728]{0:T(1024)(128)(4,1)S(1)}, s32[]{:S(2)}) async-start(s8[11534336]{0:T(1024)(128)(4,1)} %bitcast.294), calls=%async_computation.12 | async-start | bytes 6291456
  819.3 5.7 copy-start.2
  819.3 5.7 copy-start.7
  819.3 5.7 copy-start.8
  819.3 5.7 copy-start.36
  819.3 5.7 copy-start.44
  821.2 306.5 %reduce-scatter.10.cloned.1.call-start = ((), (), s32[]{:S(2)}) async-start(), calls=%async_computation.8 | async-start | bytes 1081344
  (38 other events, 116.2 us)
Sparse Core Ops, SparseCore 0:
  442.5 69.3 all-gather.5
  514.0 71.3 all-gather.3
  622.6 94.9 reduce-scatter.7
  821.3 60.6 reduce-scatter.11
  884.0 138.0 reduce-scatter.9
